TPU v7x, 512 devices: a whole 4x8x8 slice. The times are simulated.
512 devices in a mesh: seq: 64 (over y_hi, z, core), mp: 8 (over y_lo, x).
Axes of the slice: x: 4, y: 8 (y_hi: 4, y_lo: 2; y = y_hi * 2 + y_lo), z: 8, core: 2. Of those that a mesh axis runs over, the one named last changes fastest.
Arguments:
- queries: bfloat16 [16384, 8, 64], P('seq', 'mp'), may hold values from -6 to 6
- key_value: bfloat16 [16384, 8, 128], P('seq', 'mp'), may hold values from -6 to 6
- tile_fill: int32 [128], P('seq'), may hold values from 0 to 128, as said below
- out_weight: bfloat16 [8, 64, 768], P('mp'), may hold values from -0.75 to 0.75
- grad_output: bfloat16 [16384, 768], P('seq'), may hold values from -6 to 6
Outputs:
- attention_out: bfloat16 [16384, 768], P('seq')
- query_grad: float32 [16384, 8, 64], P('seq', 'mp')
- key_value_grad: float32 [16384, 8, 128], P('seq', 'mp')
- out_weight_grad: float32 [8, 64, 768], P('mp')
Inputs may be any that keep to these rules, and one draw needn't show every extreme that they name: `tile_fill`: tile 0 is full, and the first tile of every block of 256 slots holds at least one active voxel.
All inputs are finite; a program needn't handle non-finite values.
Results may differ from a plain program's by a relative error of at most 0.03.
Values may be sent and summed in bfloat16 or wider, within the bound.
A program may use at most 64 MiB of HBM per device.

v0:
```python
import jax
import jax.numpy as jnp
from jax import lax
from jax.sharding import PartitionSpec as P

TILE = 128


big_negative = -1e30


def live_slots(tile_fill, tile_rows):
    within = lax.iota(jnp.int32, tile_rows)
    return (within[None, :] < tile_fill[:, None]).reshape(-1)


def over_blocks(advance, carried, pieces):
    total_rows = pieces[0].shape[0]
    block_rows = total_rows
    while block_rows > 2048 and block_rows % 2 == 0:
        block_rows = block_rows // 2
    number = total_rows // block_rows

    def one_turn(turn_index, running):
        sliced = tuple(
            (
                lax.dynamic_slice_in_dim(member, turn_index * block_rows, block_rows, 0)
                for member in pieces
            )
        )
        return advance(running, sliced)

    return lax.fori_loop(0, number, one_turn, carried)


def shards(queries, key_value, tile_fill, out_weight, grad_output):
    head_dim = queries.shape[2]
    heads_here = queries.shape[1]
    local_rows = queries.shape[0]
    score_scale = head_dim ** (-0.5)
    live_mask = live_slots(tile_fill, TILE)
    key_live = live_mask.astype(jnp.bfloat16)
    local_keys = key_value[:, :, :head_dim]
    local_values = key_value[:, :, head_dim:]

    def forward_block(carried, pieces):
        running_max, totals, weighted = carried
        pair_block, live_block = pieces
        usable = (live_block > 0)[None, None, :]
        scores = (
            jnp.einsum(
                "qhd,khd->hqk",
                queries,
                pair_block[:, :, :head_dim],
                preferred_element_type=jnp.float32,
            )
            * score_scale
        )
        block_max = jnp.max(jnp.where(usable, scores, big_negative), axis=2)
        new_max = jnp.maximum(running_max, block_max)
        exp_rows = jnp.where(usable, jnp.exp(scores - new_max[:, :, None]), 0.0)
        factor = jnp.exp(running_max - new_max)
        totals = totals * factor + jnp.sum(exp_rows, axis=2)
        weighted = weighted * factor[:, :, None] + jnp.einsum(
            "hqk,khd->hqd",
            exp_rows.astype(jnp.bfloat16),
            pair_block[:, :, head_dim:],
            preferred_element_type=jnp.float32,
        )
        return (new_max, totals, weighted)

    start_state = (
        jnp.full((heads_here, local_rows), big_negative, jnp.float32),
        jnp.zeros((heads_here, local_rows), jnp.float32),
        jnp.zeros((heads_here, local_rows, head_dim), jnp.float32),
    )
    final_state = over_blocks(
        forward_block,
        start_state,
        (
            lax.all_gather(key_value, "seq", axis=0, tiled=True),
            lax.all_gather(key_live, "seq", axis=0, tiled=True),
        ),
    )
    row_max, totals, weighted = final_state
    attended = (weighted / totals[:, :, None]).astype(jnp.bfloat16)
    log_total = row_max + jnp.log(totals)
    live_float = live_mask.astype(jnp.float32)
    head_terms = jnp.einsum("hqd,hde->qe", attended, out_weight, preferred_element_type=jnp.float32)
    projected = lax.psum(head_terms.astype(jnp.bfloat16), "mp").astype(jnp.float32)
    attention_out = (projected * live_float[:, None]).astype(jnp.bfloat16)
    grad_mixed = grad_output * live_mask[:, None].astype(jnp.bfloat16)
    grad_attn = jnp.einsum(
        "qe,hde->qhd", grad_mixed, out_weight, preferred_element_type=jnp.float32
    ).astype(jnp.bfloat16)
    weight_terms = jnp.einsum(
        "hqd,qe->hde", attended, grad_mixed, preferred_element_type=jnp.float32
    )
    attended_rows = jnp.transpose(attended, (1, 0, 2))
    inner_rows = jnp.sum(grad_attn.astype(jnp.float32) * attended_rows.astype(jnp.float32), axis=2)
    inner_heads = inner_rows.T
    log_rows = log_total.T

    def query_grad_block(carried, pieces):
        pair_block, live_block = pieces
        usable = (live_block > 0)[None, None, :]
        scores = (
            jnp.einsum(
                "qhd,khd->hqk",
                queries,
                pair_block[:, :, :head_dim],
                preferred_element_type=jnp.float32,
            )
            * score_scale
        )
        prob_rows = jnp.where(usable, jnp.exp(scores - log_total[:, :, None]), 0.0)
        grad_probs = jnp.einsum(
            "qhd,khd->hqk",
            grad_attn,
            pair_block[:, :, head_dim:],
            preferred_element_type=jnp.float32,
        )
        grad_scores = (prob_rows * (grad_probs - inner_heads[:, :, None])).astype(jnp.bfloat16)
        return (
            carried
            + jnp.einsum(
                "hqk,khd->qhd",
                grad_scores,
                pair_block[:, :, :head_dim],
                preferred_element_type=jnp.float32,
            )
            * score_scale
        )

    zero_query = jnp.zeros((local_rows, heads_here, head_dim), jnp.float32)
    query_grad = over_blocks(
        query_grad_block,
        zero_query,
        (
            lax.all_gather(key_value, "seq", axis=0, tiled=True),
            lax.all_gather(key_live, "seq", axis=0, tiled=True),
        ),
    )
    whole_log, whole_inner = (
        lax.all_gather(log_rows, "seq", axis=0, tiled=True),
        lax.all_gather(inner_rows, "seq", axis=0, tiled=True),
    )
    key_usable = live_mask[None, :, None]

    def key_grad_block(carried, pieces):
        grad_keys, grad_values = carried
        bundle_block, log_block, inner_block = pieces
        remote_query = bundle_block[:, :, :head_dim]
        remote_grad = bundle_block[:, :, head_dim:]
        scores = (
            jnp.einsum("khd,phd->hkp", local_keys, remote_query, preferred_element_type=jnp.float32)
            * score_scale
        )
        prob_rows = jnp.where(key_usable, jnp.exp(scores - log_block.T[:, None, :]), 0.0)
        grad_values = grad_values + jnp.einsum(
            "hkp,phd->khd",
            prob_rows.astype(jnp.bfloat16),
            remote_grad,
            preferred_element_type=jnp.float32,
        )
        grad_probs = jnp.einsum(
            "khd,phd->hkp", local_values, remote_grad, preferred_element_type=jnp.float32
        )
        grad_scores = (prob_rows * (grad_probs - inner_block.T[:, None, :])).astype(jnp.bfloat16)
        grad_keys = (
            grad_keys
            + jnp.einsum(
                "hkp,phd->khd", grad_scores, remote_query, preferred_element_type=jnp.float32
            )
            * score_scale
        )
        return (grad_keys, grad_values)

    bundle = jnp.concatenate([queries, grad_attn], axis=2)
    zero_keys = jnp.zeros((local_rows, heads_here, head_dim), jnp.float32)
    grad_keys, grad_values = over_blocks(
        key_grad_block,
        (zero_keys, zero_keys),
        (lax.all_gather(bundle, "seq", axis=0, tiled=True), whole_log, whole_inner),
    )
    key_value_grad = jnp.concatenate([grad_keys, grad_values], axis=2)
    out_weight_grad = lax.psum(weight_terms, "seq")
    return (attention_out, query_grad, key_value_grad, out_weight_grad)


def solution(mesh):
    return jax.shard_map(
        shards,
        mesh=mesh,
        in_specs=(
            P("seq", "mp", None),
            P("seq", "mp", None),
            P("seq"),
            P("mp", None, None),
            P("seq", None),
        ),
        out_specs=(P("seq", None), P("seq", "mp", None), P("seq", "mp", None), P("mp", None, None)),
        check_vma=False,
    )
```

profile of v0, /device:TPU:1, one launch (start us, length us, event | category | flops | bytes accessed | tf_op | source)
XLA Modules:
  0.0 832.5 jit_solution(2396706892023930020)
XLA Ops:
  9.7 92.0 %all-gather.2 = bf16[64,1,256]{2,1,0:T(2,128)(2,1)S(1)} all-gather(bf16[1,1,256]{2,1,0:T(2,128)(2,1)S(1)} %reshape.245), channel_id=1, replica_groups=mesh['seq'=64,'mp'=8] {'seq'}, dimensions={0}, use_global_device_ids=true | all-gather | bytes 33280 | tf_op jit(solution)/shard_map/all_gather | solution.py:82
  101.8 3.5 all-gather.7.cloned.1.call-done
  105.3 29.8 %while.48 = (s32[]{:T(128)}, f32[1,256]{1,0:T(1,128)S(1)}, f32[1,256]{1,0:T(1,128)S(1)}, f32[1,256,64]{1,2,0:T(8,128)S(1)}, bf16[16384]{0:T(1024)(128)(2,1)S(1)}...) while((s32[]{:T(128)}, f32[1,256]{1,0:T(1,128)S(1)}, ...), condition=%wide.region_3.4_spmd.clone, body=%wide.region_0.3_spmd.clone.sunk | while | flops 138992896 | bytes 7008467 | solution.py:33
  138.2 79.7 %all-gather.3 = f32[64,1,256]{2,1,0:T(1,128)S(1)} all-gather(f32[1,1,256]{2,1,0:T(1,128)S(1)} %bitcast.168), channel_id=3, replica_groups=mesh['seq'=64,'mp'=8] {'seq'}, dimensions={0}, use_global_device_ids=true | all-gather | bytes 66560 | tf_op jit(solution)/shard_map/all_gather | solution.py:146
  217.9 77.2 %all-gather = f32[1,16384]{1,0:T(1,128)S(1)} all-gather(f32[1,256]{1,0:T(1,128)S(1)} %log_add_fusion), channel_id=2, replica_groups=mesh['seq'=64,'mp'=8] {'seq'}, dimensions={1}, use_global_device_ids=true | all-gather | bytes 66560 | tf_op jit(solution)/shard_map/all_gather | solution.py:145
  296.0 29.4 %while.49 = (s32[]{:T(128)}, f32[256,1,64]{0,2,1:T(8,128)S(1)}, bf16[16384,1,128]{0,2,1:T(8,128)(2,1)}, bf16[16384]{0:T(1024)(128)(2,1)S(1)}, bf16[256,1,64]{0,2...) while((s32[]{:T(128)}, f32[256,1,64]{0,2,1:T(8,128)S(1)}, ...), condition=%wide.region_7.8_spmd.clone, body=%wide.region_6.7_spmd.clone.sunk | while | flops 204527616 | bytes 5189840 | solution.py:33
  296.0 1.8 fusion.83
  297.8 1.9 fusion.84
  299.7 1.8 fusion.83
  301.5 1.9 fusion.84
  305.2 1.9 fusion.84
  307.1 1.8 fusion.83
  308.8 1.9 fusion.84
  310.8 1.8 fusion.83
  312.5 1.9 fusion.84
  314.4 1.8 fusion.83
  316.2 1.9 fusion.84
  318.1 1.8 fusion.83
  319.9 1.9 fusion.84
  321.8 1.8 fusion.83
  323.6 1.9 fusion.84
  325.5 1.9 multiply_convert_fusion
  327.4 38.8 %while.50 = (s32[]{:T(128)}, f32[256,1,64]{0,2,1:T(8,128)S(1)}, f32[256,1,64]{0,2,1:T(8,128)S(1)}, bf16[16384,1,128]{0,2,1:T(8,128)(2,1)}, bf16[256,1,64]{0,2,1:...) while((s32[]{:T(128)}, f32[256,1,64]{0,2,1:T(8,128)S(1)}, ...), condition=%wide.region_9.10_spmd.clone, body=%wide.region_8.9_spmd.clone.sunk | while | flops 272187648 | bytes 7719657 | solution.py:33
  329.1 1.9 fusion.89
  333.9 1.9 fusion.89
  338.7 1.9 fusion.89
  343.6 1.9 fusion.89
  348.4 1.9 fusion.89
  353.3 1.9 fusion.89
  358.1 1.9 fusion.89
  363.0 1.9 fusion.89
  367.3 457.0 %all-reduce.5.cloned.1.call-done = f32[1,64,768]{2,1,0:T(8,128)} async-done(((f32[1,64,768]{2,1,0:T(8,128)}), f32[1,64,768]{2,1,0:T(8,128)}) %all-reduce.5.cloned.1.call-update) | async-done | bytes 196624 | tf_op jit(solution)/shard_map/psum | solution.py:187
  (140 shorter events, 64.0 us)
Async XLA Ops:
  7.2 128.0 %copy-start = (bf16[1,64,768]{2,1,0:T(8,128)(2,1)S(1)}, bf16[1,64,768]{2,1,0:T(8,128)(2,1)}, u32[]{:S(2)}) copy-start(bf16[1,64,768]{2,1,0:T(8,128)(2,1)} %param.14) | copy-start | bytes 294916
  7.2 98.1 %all-gather.7.cloned.1.call-start = ((), (), s32[]{:S(2)}) async-start(), calls=%async_computation | async-start | bytes 4259840 | tf_op jit(solution)/shard_map/all_gather | solution.py:81
  8.8 316.7 %all-reduce.3.cloned.1.call-start = ((), (), s32[]{:S(2)}) async-start(), calls=%async_computation.1 | async-start | bytes 786432 | tf_op jit(solution)/shard_map/psum | solution.py:90
  105.3 29.9 %copy-start.3 = (bf16[256,768]{1,0:T(8,128)(2,1)S(1)}, bf16[256,768]{1,0:T(8,128)(2,1)}, u32[]{:S(2)}) copy-start(bf16[256,768]{1,0:T(8,128)(2,1)} %param.15) | copy-start | bytes 1179652
  135.2 3.0 copy-start.2
  135.2 160.8 %copy-start.4 = (bf16[256,1,64]{0,2,1:T(8,128)(2,1)S(1)}, bf16[256,1,64]{0,2,1:T(8,128)(2,1)}, u32[]{:S(2)}) copy-start(bf16[256,1,64]{0,2,1:T(8,128)(2,1)} %get-tuple-element.891) | copy-start | bytes 98308
  136.6 190.7 %all-gather.9.cloned.1.call-start = ((), (), s32[]{:S(2)}) async-start(), calls=%async_computation.2 | async-start | bytes 4259840 | tf_op jit(solution)/shard_map/all_gather | solution.py:184
  138.1 686.2 %all-reduce.5.cloned.1.call-start = ((), (), s32[]{:S(2)}) async-start(), calls=%async_computation.3 | async-start | bytes 393216 | tf_op jit(solution)/shard_map/psum | solution.py:187
  296.0 31.4 %copy-start.5 = (s32[2]{0:T(128)S(1)}, s32[2]{0:T(128)}, u32[]{:S(2)}) copy-start(s32[2]{0:T(128)} %param.13) | copy-start | bytes 28
  325.4 1.9 copy-start.1
Sparse Core Ops, SparseCore 0:
  11.7 93.5 all-gather.6
  136.8 73.9 all-reduce.2
  214.5 92.6 all-gather.8
  325.6 498.7 all-reduce.4
where the time goes:
time: 835 us; the launch traced here: 832 us
  waiting for transfers between devices  461 us (55%)
  blocking collectives  249 us (30%)
  matrix products  94.5 us (11%)
  between operations  13.9 us (2%)
  other arithmetic  9.9 us (1%)
    psum x1, waiting for transfers between devices, shards(): out_weight_grad = lax.psum(weight_terms, 'seq')  457 us
    all_gather x1, blocking collectives, shards(): lax.all_gather(key_live, 'seq', axis=0, tiled=True)  92 us
    all_gather x1, blocking collectives, shards(): lax.all_gather(inner_rows, 'seq', axis=0, tiled=True)  79.7 us
    all_gather x1, blocking collectives, shards(): lax.all_gather(log_rows, 'seq', axis=0, tiled=True)  77.2 us
  transfers between devices with their start and end apart: 4, of which 2 were waited for; matrix products, arithmetic and copies ran while one was open for 9% of the time, Pallas kernels for 0%

commit v1 on v0

v1 whole, which is shorter than its diff:
```python
import functools

import jax
import jax.numpy as jnp
from jax import lax
from jax.experimental import pallas as pl
from jax.experimental.pallas import tpu as pltpu
from jax.sharding import PartitionSpec as P

MESH = pl.DeviceIdType.MESH
BF = jnp.bfloat16
F32 = jnp.float32
TILE = 128
DH = 64
CORES = 2


def nn(a, b):
    return jnp.dot(a, b, preferred_element_type=F32)


def nt(a, b):
    return lax.dot_general(a, b, (((1,), (1,)), ((), ())), preferred_element_type=F32)


def place(offset, size):
    o = offset % size
    if o > size // 2:
        o -= size
    return 2 * o - 1 if o > 0 else -2 * o


def offset_of(rank):
    half = (rank + 1) // 2
    return half if rank % 2 == 1 else -half


def kernel(
    NY, NZ, NMP,
    fill_ref, qT_ref, kv_ref, w_ref, g_ref,
    out_ref, dq_ref, dkv_ref, wg_ref,
    kvb, kvT, qd, qS, dO, p, mh, m, oacc, ab,
    sA, sB, uoA, uoB, dsA, dsB,
    stl, str_, Lg, Dg, osend, orecv, dkacc, dsend, drecv, dqacc, dqsend, dqrecv,
    gmb, wall, attall, wg1s, wg1r, wg2, wg3,
    kv_s, kv_r, q_s, q_r, rl_s, st_s, st_r, o_s, o_r, dk_s, dk_r, dq_s, dq_r,
    w_s, w_r, at_s, at_r, g1_s, g1_r, g2_s, g2_r, g3_s, g3_r,
):
    T = kv_ref.shape[0]
    D = w_ref.shape[1]
    NB, NQ = NZ, NY * CORES
    U = NQ // 2
    RW = DH // NQ

    seq = lax.axis_index("seq")
    mp = lax.axis_index("mp")
    core = seq % CORES
    z = (seq // CORES) % NZ
    y = seq // (CORES * NZ)

    def zdev(o):
        return ((y * NZ + (z + o + NZ) % NZ) * CORES + core, mp)

    def qoff(i):
        return offset_of(i // 2) % NY, i % 2

    def qdev(i):
        dy, dc = qoff(i)
        return ((((y + dy) % NY) * NZ + z) * CORES + (core + dc) % 2, mp)

    def qabs(i):
        dy, dc = qoff(i)
        return ((y + dy) % NY) * CORES + (core + dc) % 2

    def qback(i):
        dy, dc = qoff(i)
        return 2 * place(-dy, NY) + dc

    def mdev(r):
        return (seq, (mp + r) % NMP)

    partner = qdev(1)

    def rcopy(src, dst, ssem, rsem, dev):
        return pltpu.make_async_remote_copy(
            src_ref=src, dst_ref=dst, send_sem=ssem, recv_sem=rsem, device_id=dev, device_id_type=MESH
        )

    barrier = pltpu.get_barrier_semaphore()
    for j in range(1, NB):
        pl.semaphore_signal(barrier, inc=1, device_id=zdev(offset_of(j)), device_id_type=MESH)
    for i in range(1, NQ):
        pl.semaphore_signal(barrier, inc=1, device_id=qdev(i), device_id_type=MESH)
    for r in range(1, NMP):
        pl.semaphore_signal(barrier, inc=1, device_id=mdev(r), device_id_type=MESH)

    rows = lax.broadcasted_iota(jnp.int32, (T, 1), 0)
    fills = [fill_ref[t] for t in range(T // TILE)]
    live_col = jnp.zeros((T, 1), F32)
    for t in range(T // TILE):
        inside = (rows >= t * TILE) & (rows < t * TILE + fills[t])
        live_col = jnp.where(inside, 1.0, live_col)
    lanes = lax.broadcasted_iota(jnp.int32, (1, T), 1)
    live_row = jnp.zeros((1, T), F32)
    for t in range(T // TILE):
        inside = (lanes >= t * TILE) & (lanes < t * TILE + fills[t])
        live_row = jnp.where(inside, 1.0, live_row)
    kv = kv_ref[...].astype(F32)
    is_key = lax.broadcasted_iota(jnp.int32, (1, 2 * DH), 1) < DH
    stand_in = jnp.where(is_key, kv[0:1, :], 0.0)
    kvb[0, 0:T, :] = jnp.where(live_col > 0.0, kv, stand_in).astype(BF)
    tail_rows = lax.broadcasted_iota(jnp.int32, (16, 1), 0)
    tail = jnp.zeros((16, TILE), F32)
    for t in range(T // TILE):
        tail = jnp.where(tail_rows == t, live_row[:, t * TILE : (t + 1) * TILE], tail)
    kvb[0, T : T + 16, :] = tail.astype(BF)

    pl.semaphore_wait(barrier, (NB - 1) + (NQ - 1) + (NMP - 1))

    kv_copies = []
    for j in range(1, NB):
        o = offset_of(j)
        back = place(-o, NZ)
        c = rcopy(kvb.at[0], kvb.at[back], kv_s.at[j], kv_r.at[back], zdev(o))
        c.start()
        kv_copies.append(c)

    gmb[...] = (g_ref[...].astype(F32) * live_col).astype(BF)
    qd[0, 0:DH, :] = (qT_ref[...].astype(F32) * (DH**-0.5)).astype(BF)
    qd[0, DH : 2 * DH, :] = nt(w_ref[...], gmb[...]).astype(BF)

    q_copies = []
    c = rcopy(qd.at[0], qd.at[1], q_s.at[1], q_r.at[1], partner)
    c.start()
    q_copies.append(c)
    for k in range(1, NY):
        i = 2 * k
        back = qback(i)
        c = rcopy(qd.at[0], qd.at[back], q_s.at[i], q_r.at[back], qdev(i))
        c.start()
        q_copies.append(c)

    def prepare_keys(j):
        live16 = kvb[j, T : T + 16, :].astype(F32)
        row = jnp.concatenate([live16[t : t + 1, :] for t in range(T // TILE)], axis=1)
        kvT[j, 0 : 2 * DH, :] = (kvb[j, 0:T, :].astype(F32).T * row).astype(BF)
        kvT[j, 2 * DH : 2 * DH + 16, :] = jnp.broadcast_to(row, (16, T)).astype(BF)

    def prepare_queries(i):
        qS[i, 0:DH, :] = qd[i, 0:DH, :]
        dO[i] = qd[i, DH : 2 * DH, :]

    for i in range(NQ):
        m[i] = jnp.full((8, T), -1e30, F32)
        oacc[i] = jnp.zeros((DH + 16, T), F32)
        dqacc[i] = jnp.zeros((DH, T), F32)
        qS[i, DH : 2 * DH, :] = jnp.zeros((DH, T), BF)
    for t in range(U):
        uoA[t, 0:DH, :] = jnp.zeros((DH, T), BF)
        uoB[t, 0:DH, :] = jnp.zeros((DH, T), BF)
    prepare_keys(0)
    prepare_queries(0)

    for k in range(1, NY):
        i = 2 * k
        rcopy(qd.at[0], qd.at[i], q_s.at[i], q_r.at[i], partner).wait_recv()
        c = rcopy(qd.at[i], qd.at[i + 1], rl_s.at[i], q_r.at[i + 1], partner)
        c.start()
        q_copies.append(c)
        prepare_queries(i)

    wall[mp] = w_ref[...]
    w_copies = []
    for r in range(1, NMP):
        c = rcopy(wall.at[mp], wall.at[mp], w_s.at[r], w_r.at[r], mdev(r))
        c.start()
        w_copies.append(c)

    for k in range(NY):
        i = 2 * k + 1
        rcopy(qd.at[0], qd.at[i], q_s.at[i], q_r.at[i], partner).wait_recv()
        prepare_queries(i)

    def S(j, half, buf):
        for t in range(U):
            buf[t] = nn(kvb[j, 0:T, :], qS[half * U + t])

    def E(j, half, buf):
        for t in range(U):
            i = half * U + t
            m_old = m[i, 0:1, :]
            m_new = jnp.maximum(m_old, jnp.max(buf[t], axis=0, keepdims=True))
            mh[j, i, 0:1, :] = m_new
            m[i, 0:1, :] = m_new
            ab[half, t, 0:1, :] = jnp.exp(m_old - m_new)
            p[j, i] = jnp.exp(buf[t] - m_new).astype(BF)

    def O(j, half):
        for t in range(U):
            i = half * U + t
            oacc[i] = oacc[i] * ab[half, t, 0:1, :] + nn(kvT[j, DH : 2 * DH + 16, :], p[j, i])

    S(0, 0, sA)
    E(0, 0, sA)
    S(0, 1, sB)

    @pl.loop(1, NB)
    def _(j):
        rcopy(kvb.at[0], kvb.at[j], kv_s.at[j], kv_r.at[j], partner).wait_recv()
        prepare_keys(j)
        S(j, 0, sA)
        E(j - 1, 1, sB)
        O(j - 1, 0)
        S(j, 1, sB)
        E(j, 0, sA)
        O(j - 1, 1)

    E(NB - 1, 1, sB)
    O(NB - 1, 0)
    O(NB - 1, 1)

    for i in range(NQ):
        acc = oacc[i]
        total = acc[DH : DH + 1, :]
        o = acc[0:DH, :] * (1.0 / total)
        osend[i] = o.astype(BF)
        row = qabs(i)
        stl[pl.ds(row, 1), :] = m[i, 0:1, :] + jnp.log(total)
        stl[pl.ds(NQ + row, 1), :] = jnp.sum(o * dO[i].astype(F32), axis=0, keepdims=True)

    st_copies = []
    for i in range(1, NQ):
        back = qback(i)
        c = rcopy(stl, str_.at[back], st_s.at[i], st_r.at[back], qdev(i))
        c.start()
        st_copies.append(c)
    o_copies = []
    for i in range(1, NQ):
        back = qback(i)
        c = rcopy(osend.at[i], orecv.at[back], o_s.at[i], o_r.at[back], qdev(i))
        c.start()
        o_copies.append(c)
    str_[0] = stl[...]
    for i in range(1, NQ):
        rcopy(stl, str_.at[i], st_s.at[i], st_r.at[i], partner).wait_recv()
    big = str_[0, 0:NQ, :]
    for s in range(1, NQ):
        big = jnp.maximum(big, str_[s, 0:NQ, :])
    wsum = jnp.zeros((NQ, T), F32)
    dsum = jnp.zeros((NQ, T), F32)
    for s in range(NQ):
        wt = jnp.exp(str_[s, 0:NQ, :] - big)
        wsum = wsum + wt
        dsum = dsum + wt * str_[s, NQ : 2 * NQ, :]
    stl2 = big + jnp.log(wsum)
    Lg[NQ, 0:NQ, :] = stl2
    Dg[NQ, 0:NQ, :] = dsum / wsum
    for i in range(NQ):
        Lg[i, 0:1, :] = Lg[NQ, pl.ds(qabs(i), 1), :]
        Dg[i, 0:1, :] = Dg[NQ, pl.ds(qabs(i), 1), :]

    def Ust(j, half, buf, uo):
        for t in range(U):
            i = half * U + t
            c = jnp.exp(mh[j, i, 0:1, :] - Lg[i, 0:1, :])
            cdo = (dO[i].astype(F32) * c).astype(BF)
            uo[t, DH : 2 * DH, :] = cdo
            rhs = jnp.concatenate([jnp.zeros((DH, T), BF), cdo], axis=0)
            buf[t] = nn(kvb[j, 0:T, :], rhs) - c * Dg[i, 0:1, :]

    def Dst(j, half, buf, ds):
        for t in range(U):
            ds[t] = (p[j, half * U + t].astype(F32) * buf[t]).astype(BF)

    def Mst(j, half, ds, uo):
        acc = None
        for t in range(U):
            i = half * U + t
            dqacc[i] += nn(kvT[j, 0:DH, :], ds[t])
            r = nt(ds[t], qS[i]) + nt(p[j, i], uo[t])
            acc = r if acc is None else acc + r
        if half == 0:
            dkacc[...] = acc
        else:
            dkacc[...] += acc

    def dk_copy(j):
        half = (j + 1) // 2
        odd = j % 2
        o = (2 * odd - 1) * half
        back = jnp.where(half * 2 == NZ, j, j + 2 * odd - 1)
        return rcopy(dsend.at[j], drecv.at[back], dk_s.at[j], dk_r.at[back], zdev(o))

    def turn(n):
        done = n + 1
        Mst(done, 0, dsA, uoA)
        Dst(done, 1, sB, dsB)
        Ust(n, 0, sA, uoA)
        Mst(done, 1, dsB, uoB)
        dsend[done] = dkacc[...].astype(BF)
        dk_copy(done).start()
        Dst(n, 0, sA, dsA)
        Ust(n, 1, sB, uoB)

    Ust(NB - 1, 0, sA, uoA)
    Dst(NB - 1, 0, sA, dsA)
    Ust(NB - 1, 1, sB, uoB)

    first = (NB - 1) // 2

    @pl.loop(0, first)
    def _(t):
        turn(NB - 2 - t)

    att = jnp.zeros((DH, T), F32)
    for i in range(1, NQ):
        rcopy(osend.at[i], orecv.at[i], o_s.at[i], o_r.at[i], partner).wait_recv()
    orecv[0] = osend[0]
    for s in range(NQ):
        wt = jnp.exp(str_[s, pl.ds(qabs(0), 1), :] - Lg[0, 0:1, :])
        att = att + wt * orecv[s].astype(F32)
    attall[mp] = (att * live_row).astype(BF)
    at_copies = []
    for r in range(1, NMP):
        c = rcopy(attall.at[mp], attall.at[mp], at_s.at[r], at_r.at[r], mdev(r))
        c.start()
        at_copies.append(c)
    wgp = nn(att.astype(BF), gmb[...])
    for s in range(NQ):
        wg1s[s] = wgp[s * RW : (s + 1) * RW, :].astype(BF)
    g1_copies = []
    for i in range(1, NQ):
        back = qback(i)
        c = rcopy(wg1s.at[qabs(i)], wg1r.at[back], g1_s.at[i], g1_r.at[back], qdev(i))
        c.start()
        g1_copies.append(c)

    @pl.loop(first, NB - 1)
    def _(t):
        turn(NB - 2 - t)

    Mst(0, 0, dsA, uoA)
    Dst(0, 1, sB, dsB)
    Mst(0, 1, dsB, uoB)

    dq_copies = []
    for i in range(1, NQ):
        dqsend[i] = (dqacc[i] * (DH**-0.5)).astype(BF)
        back = qback(i)
        c = rcopy(dqsend.at[i], dqrecv.at[back], dq_s.at[i], dq_r.at[back], qdev(i))
        c.start()
        dq_copies.append(c)

    wg1r[0] = wg1s[qabs(0)]
    for i in range(1, NQ):
        rcopy(wg1s.at[0], wg1r.at[i], g1_s.at[i], g1_r.at[i], partner).wait_recv()
    part = wg1r[0].astype(F32)
    for i in range(1, NQ):
        part = part + wg1r[i].astype(F32)
    wg2[z] = part.astype(BF)
    g2_copies = []
    for r in range(1, NZ):
        c = rcopy(wg2.at[z], wg2.at[z], g2_s.at[r], g2_r.at[r], zdev(r))
        c.start()
        g2_copies.append(c)

    for r in range(1, NMP):
        rcopy(wall.at[0], wall.at[0], w_s.at[r], w_r.at[r], partner).wait_recv()
        rcopy(attall.at[0], attall.at[0], at_s.at[r], at_r.at[r], partner).wait_recv()
    att_rows = attall[...].reshape(NMP * DH, T).astype(F32).T.astype(BF)
    out_ref[...] = nn(att_rows, wall[...].reshape(NMP * DH, D)).astype(BF)

    for r in range(1, NZ):
        rcopy(wg2.at[0], wg2.at[0], g2_s.at[r], g2_r.at[r], partner).wait_recv()
    part = wg2[0].astype(F32)
    for k in range(1, NZ):
        part = part + wg2[k].astype(F32)
    own = qabs(0)
    wg3[own] = part.astype(BF)
    g3_copies = []
    for i in range(1, NQ):
        back = qback(i)
        c = rcopy(wg3.at[own], wg3.at[own], g3_s.at[i], g3_r.at[back], qdev(i))
        c.start()
        g3_copies.append(c)

    total = dqacc[0] * (DH**-0.5)
    for i in range(1, NQ):
        rcopy(dqsend.at[i], dqrecv.at[i], dq_s.at[i], dq_r.at[i], partner).wait_recv()
        total = total + dqrecv[i].astype(F32)
    dq_ref[...] = total

    total = dkacc[...]
    for j in range(1, NB):
        rcopy(dsend.at[j], drecv.at[j], dk_s.at[j], dk_r.at[j], partner).wait_recv()
        total = total + drecv[j].astype(F32)
    dkv_ref[...] = total * live_col

    for i in range(1, NQ):
        rcopy(wg3.at[0], wg3.at[0], g3_s.at[i], g3_r.at[i], partner).wait_recv()
    for s in range(NQ):
        wg_ref[s * RW : (s + 1) * RW, :] = wg3[s].astype(F32)

    for c in (
        kv_copies + q_copies + w_copies + st_copies + o_copies + at_copies + g1_copies + dq_copies + g2_copies + g3_copies
    ):
        c.wait_send()
    for j in range(1, NB):
        rcopy(dsend.at[j], drecv.at[j], dk_s.at[j], dk_r.at[j], partner).wait_send()


def solution(mesh):
    NMP = mesh.shape["mp"]
    NSEQ = mesh.shape["seq"]
    NY, NZ = {64: (4, 8), 8: (2, 2), 16: (2, 4)}[NSEQ]
    NB, NQ = NZ, NY * CORES
    U = NQ // 2

    def shards(queries, key_value, tile_fill, out_weight, grad_output):
        T = queries.shape[0]
        D = out_weight.shape[2]
        qT = queries[:, 0, :].T
        kv = key_value[:, 0, :]
        w = out_weight[0]
        V = pl.BlockSpec(memory_space=pltpu.VMEM)
        v = pltpu.VMEM
        dma = lambda n: pltpu.SemaphoreType.DMA((n,))
        RW = DH // NQ
        scratch = [
            v((NB, T + 16, 2 * DH), BF), v((NB, 2 * DH + 16, T), BF), v((NQ, 2 * DH, T), BF), v((NQ, 2 * DH, T), BF),
            v((NQ, DH, T), BF), v((NB, NQ, T, T), BF), v((NB, NQ, 8, T), F32), v((NQ, 8, T), F32),
            v((NQ, DH + 16, T), F32), v((2, U, 8, T), F32),
            v((U, T, T), F32), v((U, T, T), F32), v((U, 2 * DH, T), BF), v((U, 2 * DH, T), BF),
            v((U, T, T), BF), v((U, T, T), BF),
            v((2 * NQ, T), F32), v((NQ, 2 * NQ, T), F32), v((NQ + 1, 8, T), F32), v((NQ + 1, 8, T), F32),
            v((NQ, DH, T), BF), v((NQ, DH, T), BF), v((T, 2 * DH), F32), v((NB, T, 2 * DH), BF), v((NB, T, 2 * DH), BF),
            v((NQ, DH, T), F32), v((NQ, DH, T), BF), v((NQ, DH, T), BF),
            v((T, D), BF), v((NMP, DH, D), BF), v((NMP, DH, T), BF),
            v((NQ, RW, D), BF), v((NQ, RW, D), BF), v((NZ, RW, D), BF), v((NQ, RW, D), BF),
            dma(NB), dma(NB), dma(NQ), dma(NQ), dma(NQ), dma(NQ), dma(NQ), dma(NQ), dma(NQ),
            dma(NB), dma(NB), dma(NQ), dma(NQ),
            dma(NMP), dma(NMP), dma(NMP), dma(NMP), dma(NQ), dma(NQ), dma(NZ), dma(NZ), dma(NQ), dma(NQ),
        ]
        out, dqT, dkv, wg = pl.pallas_call(
            functools.partial(kernel, NY, NZ, NMP),
            name="voxel_attention",
            out_shape=[
                jax.ShapeDtypeStruct((T, D), BF),
                jax.ShapeDtypeStruct((DH, T), F32),
                jax.ShapeDtypeStruct((T, 2 * DH), F32),
                jax.ShapeDtypeStruct((DH, D), F32),
            ],
            in_specs=[pl.BlockSpec(memory_space=pltpu.SMEM), V, V, V, V],
            out_specs=[V, V, V, V],
            scratch_shapes=scratch,
            compiler_params=pltpu.CompilerParams(
                collective_id=0, has_side_effects=True, vmem_limit_bytes=60 * 1024 * 1024
            ),
        )(tile_fill, qT, kv, w, grad_output)
        return out, dqT.T[:, None, :], dkv[:, None, :], wg[None]

    return jax.shard_map(
        shards,
        mesh=mesh,
        in_specs=(
            P("seq", "mp", None),
            P("seq", "mp", None),
            P("seq"),
            P("mp", None, None),
            P("seq", None),
        ),
        out_specs=(P("seq", None), P("seq", "mp", None), P("seq", "mp", None), P("mp", None, None)),
        check_vma=False,
    )
```

time: 835 us -> 75.4 us (0.09)
  waiting for transfers between devices: 461 us -> 0 us
  blocking collectives: 249 us -> 0 us
  matrix products: 94.5 us -> 0 us
  Pallas kernels: 0 us -> 70.8 us
  between operations: 13.9 us -> 0.66 us
  other arithmetic: 9.9 us -> 0 us
    psum x2 -> x0, waiting for transfers between devices: 457 us -> none  [the longest x1 457 us: shards(): out_weight_grad = lax.psum(weight_terms, 'seq')]
    all_gather x3 -> x0, blocking collectives: 249 us -> none  [the longest x1 92 us: shards(): lax.all_gather(key_live, 'seq', axis=0, tiled=True)]
    dot_general x59 -> x0, matrix products: 94.5 us -> none  [the longest x8 15 us: key_grad_block(): jnp.einsum('hkp,phd->khd', grad_scores, remote_query, preferred_element_t...]
    pallas_call x0 -> x1, Pallas kernels: none -> 70.8 us  [shards(): pl.pallas_call(functools.partial(kernel, NY, NZ, NMP), name='voxel_attent...]
  transfers between devices with their start and end apart: 4 -> 0, of which waited for: 2 -> 0; matrix products, arithmetic and copies ran while one was open for 9% -> 0% of each run, Pallas kernels for 0% -> 0%
where the time goes in v1:
time: 75.4 us; the launch traced here: 75.2 us
  Pallas kernels  70.8 us (94%)
  local copies, waits for them, and re-layouts  3.78 us (5%)
    pallas_call x1, Pallas kernels, shards(): pl.pallas_call(functools.partial(kernel, NY, NZ, NMP), name='voxel_attent...  70.8 us
    unnamed x10, local copies, waits for them, and re-layouts  3.78 us

profile of v1, /device:TPU:1, one launch (start us, length us, event | category | flops | bytes accessed | tf_op | source)
XLA Modules:
  0.0 75.2 jit_solution(16868889592266313008)
XLA Ops:
  0.6 70.8 %voxel_attention.1 = (bf16[256,768]{1,0:T(8,128)(2,1)}, f32[64,256]{1,0:T(8,128)}, f32[256,128]{1,0:T(8,128)}, f32[64,768]{1,0:T(8,128)}) custom-call(s32[2]{0:T(128)} %fill_ref.1, bf16[64,256]{1,0:T(8,128)(2,1)} %bitcast.17, bf16[256,128]{1,0:T(8,128)(2,1)} %bitcast.16, bf16[64,768]{1,0:T(8,128)(2,1)} %bitcast.14, bf16[256,768]{1,0:T(8,128)(2,1)} %g_ref.1), custom_call_target="tpu_custom_call" | custom-call | tf_op jit(solution)/shard_map/voxel_attention/pallas_call | solution.py:444
  71.4 0.0 copy-start.2
  71.4 0.0 copy-start.1
  71.4 1.8 %copy.14 = bf16[256,768]{1,0:T(8,128)(2,1)} copy(bf16[256,768]{1,0:T(8,128)(2,1)} %get-tuple-element.20) | data formatting | bytes 786432
  73.3 0.0 copy-done.2
  73.3 0.0 copy-start
  73.3 0.6 copy.15
  73.9 0.0 copy-done.1
  73.9 0.7 copy.16
  74.5 0.0 copy-done
  74.5 0.7 copy.17
Async XLA Ops:
  71.4 1.8 %copy-start.2 = (f32[64,256]{1,0:T(8,128)S(1)}, f32[64,256]{1,0:T(8,128)}, u32[]{:S(2)}) copy-start(f32[64,256]{1,0:T(8,128)} %get-tuple-element.9) | copy-start | bytes 196612
  71.4 2.5 %copy-start.1 = (f32[256,128]{1,0:T(8,128)S(1)}, f32[256,128]{1,0:T(8,128)}, u32[]{:S(2)}) copy-start(f32[256,128]{1,0:T(8,128)} %get-tuple-element.10) | copy-start | bytes 393220
  73.3 1.3 %copy-start = (f32[64,768]{1,0:T(8,128)S(1)}, f32[64,768]{1,0:T(8,128)}, u32[]{:S(2)}) copy-start(f32[64,768]{1,0:T(8,128)} %get-tuple-element.11) | copy-start | bytes 589828

commit v2 on v1

v2 whole, which is shorter than its diff:
```python
import functools

import jax
import jax.numpy as jnp
from jax import lax
from jax.experimental import pallas as pl
from jax.experimental.pallas import tpu as pltpu
from jax.sharding import PartitionSpec as P

MESH = pl.DeviceIdType.MESH
BF = jnp.bfloat16
F32 = jnp.float32
TILE = 128
DH = 64
CORES = 2


def nn(a, b):
    return jnp.dot(a, b, preferred_element_type=F32)


def nt(a, b):
    return lax.dot_general(a, b, (((1,), (1,)), ((), ())), preferred_element_type=F32)


def place(offset, size):
    o = offset % size
    if o > size // 2:
        o -= size
    return 2 * o - 1 if o > 0 else -2 * o


def offset_of(rank):
    half = (rank + 1) // 2
    return half if rank % 2 == 1 else -half


def kernel(
    NY, NZ, NMP,
    fill_hbm, qT_hbm, kv_hbm, w_hbm, g_hbm,
    out_ref, dq_ref, dkv_ref, wg_ref,
    fill_ref, qT_ref, kv_ref, g_ref, in_sem,
    kvb, kvT, qq, dd, qS, p, mh, m, oacc, ab, ds,
    sA, sB, Ll, Dl, rr, wq,
    stl, str_, Lg, Dg, osend, orecv, dkp, dsend, drecv, dqacc, dqsend, dqrecv,
    gmb, wall, attall, wg1s, wg1r, wg2, wg3,
    kv0_s, kv_s, kv_r, q_s, q_r, ql_s, d_s, d_r, dl_s, st_s, st_r, o_s, o_r, dk_s, dk_r, dq_s, dq_r,
    w_s, w_r, wl_s, wl_r, at_s, at_r, g1_s, g1_r, g2_s, g2_r, g3_s, g3_r,
):
    T = kv_ref.shape[0]
    D = wall.shape[3]
    NB, NQ = NZ, NY * CORES
    U = NQ // 2
    H = NB // 2
    RW = DH // NQ
    YL = 2 if NMP % 2 == 0 else 1
    X = NMP // YL
    CUTS = ((0, 144), (144, 128))
    SCALE = DH**-0.5

    seq = lax.axis_index("seq")
    mp = lax.axis_index("mp")
    core = seq % CORES
    z = (seq // CORES) % NZ
    y = seq // (CORES * NZ)

    def zdev(o):
        return ((y * NZ + (z + o + NZ) % NZ) * CORES + core, mp)

    def qoff(i):
        return offset_of(i // 2) % NY, i % 2

    def qdev(i):
        dy, dc = qoff(i)
        return ((((y + dy) % NY) * NZ + z) * CORES + (core + dc) % 2, mp)

    def qabs(i):
        dy, dc = qoff(i)
        return ((y + dy) % NY) * CORES + (core + dc) % 2

    def qback(i):
        dy, dc = qoff(i)
        return 2 * place(-dy, NY) + dc

    def mdev(r):
        return (seq, (mp + r) % NMP)

    def head_at(flip, dx):
        return ((mp // X + flip) % YL) * X + (mp % X + dx + X) % X

    partner = qdev(1)

    def rcopy(src, dst, ssem, rsem, dev):
        return pltpu.make_async_remote_copy(
            src_ref=src, dst_ref=dst, send_sem=ssem, recv_sem=rsem, device_id=dev, device_id_type=MESH
        )

    barrier = pltpu.get_barrier_semaphore()
    for j in range(1, NB):
        pl.semaphore_signal(barrier, inc=1, device_id=zdev(offset_of(j)), device_id_type=MESH)
    for i in range(1, NQ):
        pl.semaphore_signal(barrier, inc=1, device_id=qdev(i), device_id_type=MESH)
    for r in range(1, NMP):
        pl.semaphore_signal(barrier, inc=1, device_id=mdev(r), device_id_type=MESH)

    w_ref = wall.at[mp]
    loads = [
        pltpu.make_async_copy(a, b, in_sem.at[n])
        for n, (a, b) in enumerate(((kv_hbm, kv_ref), (qT_hbm, qT_ref), (w_hbm, w_ref), (g_hbm, g_ref), (fill_hbm, fill_ref)))
    ]
    for c in loads:
        c.start()

    rows = lax.broadcasted_iota(jnp.int32, (T, 1), 0)
    loads[4].wait()
    fills = [fill_ref[t] for t in range(T // TILE)]
    live_col = jnp.zeros((T, 1), F32)
    for t in range(T // TILE):
        inside = (rows >= t * TILE) & (rows < t * TILE + fills[t])
        live_col = jnp.where(inside, 1.0, live_col)
    lanes = lax.broadcasted_iota(jnp.int32, (1, T), 1)
    live_row = jnp.zeros((1, T), F32)
    for t in range(T // TILE):
        inside = (lanes >= t * TILE) & (lanes < t * TILE + fills[t])
        live_row = jnp.where(inside, 1.0, live_row)
    loads[0].wait()
    kv = kv_ref[...].astype(F32)
    is_key = lax.broadcasted_iota(jnp.int32, (1, 2 * DH), 1) < DH
    stand_in = jnp.where(is_key, kv[0:1, :], 0.0)
    kvb[0, 0:T, :] = jnp.where(live_col > 0.0, kv, stand_in).astype(BF)
    tail_rows = lax.broadcasted_iota(jnp.int32, (16, 1), 0)
    tail = jnp.zeros((16, TILE), F32)
    for t in range(T // TILE):
        tail = jnp.where(tail_rows == t, live_row[:, t * TILE : (t + 1) * TILE], tail)
    kvb[0, T : T + 16, :] = tail.astype(BF)
    loads[1].wait()
    qq[0] = (qT_ref[...].astype(F32) * SCALE).astype(BF)
    loads[2].wait()
    loads[3].wait()
    gmb[...] = (g_ref[...].astype(F32) * live_col).astype(BF)
    dd[0] = nt(wall[mp].reshape(DH, D), gmb[...]).astype(BF)

    def prepare_keys(j):
        live16 = kvb[j, T : T + 16, :].astype(F32)
        row = jnp.concatenate([live16[t : t + 1, :] for t in range(T // TILE)], axis=1)
        kvT[j, 0 : 2 * DH, :] = (kvb[j, 0:T, :].astype(F32).T * row).astype(BF)
        kvT[j, 2 * DH : 2 * DH + 16, :] = jnp.broadcast_to(row, (16, T)).astype(BF)

    def prepare_queries(i):
        qS[i, 0:DH, :] = qq[i]

    prepare_keys(0)
    prepare_queries(0)
    for i in range(NQ):
        qS[i, DH : 2 * DH, :] = jnp.zeros((DH, T), BF)
        wq[i, DH : 2 * DH, :] = jnp.zeros((DH, T), BF)

    pl.semaphore_wait(barrier, (NB - 1) + (NQ - 1) + (NMP - 1))

    copies = []

    def send(src, dst, ssem, rsem, dev):
        rcopy(src, dst, ssem, rsem, dev).start()
        copies.append(lambda: (src, ssem))

    def send_row(buf, a, b, ssem, k, rsem, dev):
        rcopy(buf.at[a], buf.at[b], ssem.at[k], rsem, dev).start()
        copies.append(lambda: (buf.at[(0, 0) if isinstance(a, tuple) else 0], ssem.at[k]))

    def arrive(dst, rsem):
        rcopy(dst, dst, kv0_s.at[0], rsem, partner).wait_recv()

    def send_keys(j, hf, to, sem, k, dev):
        lo, size = CUTS[hf]
        src, dst = kvb.at[j, pl.ds(lo, size)], kvb.at[to, pl.ds(lo, size)]
        rcopy(src, dst, sem.at[k], kv_r.at[2 * to + hf], dev).start()
        copies.append(lambda: (kvb.at[0, pl.ds(lo, size)], sem.at[k]))

    right = place(-1, NZ)
    for hf in range(2):
        if NZ > 2 or hf == 0:
            send_keys(0, hf, right, kv0_s, hf, zdev(1))
        if NZ > 2 or hf == 1:
            send_keys(0, hf, 1, kv0_s, 2 + hf, zdev(-1))

    def spread(buf, ssem, rsem):
        for k in range(1, NY):
            i, back = 2 * k, qback(2 * k)
            send(buf.at[0], buf.at[back], ssem.at[i], rsem.at[back], qdev(i))
        send(buf.at[0], buf.at[1], ssem.at[1], rsem.at[1], partner)

    spread(qq, q_s, q_r)
    spread(dd, d_s, d_r)
    if YL == 2:
        send_row(wall, (mp, core), (mp, core), w_s, 0, w_r.at[0], (seq, head_at(1, 0)))
    for i in range(NQ):
        m[i] = jnp.full((8, T), -1e30, F32)
        oacc[i] = jnp.zeros((2 * DH + 16, T), F32)
        dqacc[i] = jnp.zeros((DH, T), F32)

    def relay(buf, lsem, rsem, k):
        i = 2 * k
        arrive(buf.at[i], rsem.at[i])
        send_row(buf, i, i + 1, lsem, i, rsem.at[i + 1], partner)

    def forward_keys(j, hf):
        arrive(kvb.at[j, pl.ds(*CUTS[hf])], kv_r.at[2 * j + hf])
        k = (j + 1) // 2
        odd = j % 2 == 1
        if j < NZ - 1 and (k + 1 < NZ // 2 or hf == (1 if odd else 0)):
            to = j + 2 if k + 1 < NZ // 2 else NZ - 1
            send_keys(j, hf, to, kv_s, 2 * j + hf, zdev(-1 if odd else 1))

    def before(it):
        def take(js):
            for hf in range(2):
                for j in js:
                    forward_keys(j, hf)

        js = []
        if it == 0 and H > 1:
            js = [1, 2]
        if it > 1 and it + 1 < H:
            js = [2 * it + 1, 2 * it + 2]
        if it == NB - 1:
            js = [NB - 1]
        take(js)
        if it == 0:
            for k in range(1, max(NY - 1, 1)):
                relay(qq, ql_s, q_r, k)
        for half in range(2):
            if it == half * (H // 2):
                if half == 1 and it == 0:
                    relay(qq, ql_s, q_r, NY - 1)
                for i in range(half * U, half * U + U):
                    if i % 2 == 1:
                        arrive(qq.at[i], q_r.at[i])
                    if i > 0:
                        prepare_queries(i)
        if it == 0 and H > 2:
            take([3, 4])
            js = js + [3, 4]
        if it == 0 and H // 2 > 0:
            relay(qq, ql_s, q_r, NY - 1)
        for j in js:
            prepare_keys(j)
        if it == max(NB - 5, 0):
            if YL == 2:
                arrive(wall.at[0, 0], w_r.at[0])
            for dx in range(1, X):
                for flip in range(YL):
                    k = 1 + 2 * (dx - 1) + flip
                    h = head_at(flip, 0)
                    send_row(wall, (h, core), (h, core), w_s, k, w_r.at[k], (seq, head_at(0, dx)))
        if it == max(NB - 2, 0):
            for k in range(1, NY):
                relay(dd, dl_s, d_r, k)

    def step_of(n):
        late = n - 2 * H
        if isinstance(n, int):
            j = n if n < H else (n - H if late < 0 else H + late // 2)
            return j, U * (0 if n < H else (1 if late < 0 else late % 2))
        j = jnp.where(n < H, n, jnp.where(late < 0, n - H, H + jnp.right_shift(late, 1)))
        half = jnp.where(n < H, 0, jnp.where(late < 0, 1, late & 1))
        return j, half * U

    def S(n, buf):
        j, i0 = step_of(n)
        for t in range(U):
            buf[t] = nn(kvb[j, 0:T, :], qS[i0 + t])

    def E(n, buf, par):
        j, i0 = step_of(n)
        for t in range(U):
            i = i0 + t
            m_old = m[i, 0:1, :]
            m_new = jnp.maximum(m_old, jnp.max(buf[t], axis=0, keepdims=True))
            mh[j, i, 0:1, :] = m_new
            m[i, 0:1, :] = m_new
            ab[par, t, 0:1, :] = jnp.exp(m_old - m_new)
            p[j, i] = jnp.exp(buf[t] - m_new).astype(BF)

    def O(n, par):
        j, i0 = step_of(n)
        for t in range(U):
            i = i0 + t
            oacc[i] = oacc[i] * ab[par, t, 0:1, :] + nn(kvT[j], p[j, i])

    before(0)
    first, last = 0, 2 * NB - 1
    S(first, sA)
    E(first, sA, 0)
    S(first + 1, sB)

    @pl.loop(1, NB)
    def _(it):
        for fixed in range(1, NB):
            if fixed in WAITS(NB, H):
                pl.when(it == fixed)(functools.partial(before, fixed))
        n = 2 * it
        S(n, sA)
        E(n - 1, sB, 1)
        O(n - 2, 0)
        S(n + 1, sB)
        E(n, sA, 0)
        O(n - 1, 1)

    E(last, sB, 1)
    O(last - 1, 0)
    O(last, 1)
    for k in range(NY):
        arrive(dd.at[2 * k + 1], d_r.at[2 * k + 1])

    for i in range(NQ):
        total = oacc[i, 2 * DH : 2 * DH + 1, :]
        inv = 1.0 / total
        o = oacc[i, DH : 2 * DH, :] * inv
        oacc[i, 0:DH, :] = oacc[i, 0:DH, :] * inv
        osend[i] = o.astype(BF)
        lrow = m[i, 0:1, :] + jnp.log(total)
        drow = jnp.sum(o * dd[i].astype(F32), axis=0, keepdims=True)
        Ll[i, 0:1, :] = lrow
        Dl[i, 0:1, :] = drow
        stl[pl.ds(qabs(i), 1), :] = lrow
        stl[pl.ds(NQ + qabs(i), 1), :] = drow

    for i in range(1, NQ):
        back = qback(i)
        send(stl, str_.at[back], st_s.at[i], st_r.at[back], qdev(i))
    for i in range(1, NQ):
        back = qback(i)
        send(osend.at[i], orecv.at[back], o_s.at[i], o_r.at[back], qdev(i))

    def Ust(j, half, buf):
        for t in range(U):
            i = half * U + t
            c = jnp.exp(mh[j, i, 0:1, :] - Ll[i, 0:1, :])
            rhs = jnp.concatenate([jnp.zeros((DH, T), BF), (dd[i].astype(F32) * c).astype(BF)], axis=0)
            buf[t] = nn(kvb[j, 0:T, :], rhs) - c * Dl[i, 0:1, :]

    def Dst(j, half, buf):
        for t in range(U):
            i = half * U + t
            ds[j, i] = (p[j, i].astype(F32) * buf[t]).astype(BF)

    def Mst(j, half):
        for t in range(U):
            i = half * U + t
            dqacc[i] += nn(kvT[j, 0:DH, :], ds[j, i])

    Ust(0, 0, sA)
    Dst(0, 0, sA)
    Ust(0, 1, sB)

    @pl.loop(1, NB)
    def _(j):
        Ust(j, 0, sA)
        Dst(j - 1, 1, sB)
        Mst(j - 1, 0)
        Ust(j, 1, sB)
        Dst(j, 0, sA)
        Mst(j - 1, 1)

    Dst(NB - 1, 1, sB)
    Mst(NB - 1, 0)
    Mst(NB - 1, 1)

    str_[0] = stl[...]
    for i in range(1, NQ):
        arrive(str_.at[i], st_r.at[i])
    if YL == 2:
        send_row(wall, (head_at(1, 0), core), (head_at(1, 0), core), wl_s, 0, wl_r.at[0], partner)
    for dx in range(1, X):
        for flip in range(YL):
            k = 1 + 2 * (dx - 1) + flip
            h = head_at(flip, -dx)
            arrive(wall.at[0, 0], w_r.at[k])
            send_row(wall, (h, core), (h, core), wl_s, k, wl_r.at[k], partner)
    big = str_[0, 0:NQ, :]
    for s in range(1, NQ):
        big = jnp.maximum(big, str_[s, 0:NQ, :])
    wsum = jnp.zeros((NQ, T), F32)
    dsum = jnp.zeros((NQ, T), F32)
    for s in range(NQ):
        wt = jnp.exp(str_[s, 0:NQ, :] - big)
        wsum = wsum + wt
        dsum = dsum + wt * str_[s, NQ : 2 * NQ, :]
    Lg[0:NQ, :] = big + jnp.log(wsum)
    Dg[0:NQ, :] = dsum / wsum
    for i in range(NQ):
        w = jnp.exp(Ll[i, 0:1, :] - Lg[pl.ds(qabs(i), 1), :])
        e = w * (Dl[i, 0:1, :] - Dg[pl.ds(qabs(i), 1), :])
        q32 = qq[i].astype(F32)
        wq[i, 0:DH, :] = (q32 * w).astype(BF)
        rr[i, 0:DH, :] = q32 * e
        rr[i, DH : 2 * DH, :] = dd[i].astype(F32) * w
        total = (dqacc[i] * w + oacc[i, 0:DH, :] * e) * SCALE
        if i == 0:
            dqacc[0] = total
        else:
            dqsend[i] = total.astype(BF)

    def key_pair(n):
        @pl.loop(0, 2)
        def _(b):
            j = NB - 1 - 2 * n - b
            acc = None
            for i in range(NQ):
                c = jnp.exp(mh[j, i, 0:1, :] - Ll[i, 0:1, :])
                r = nt(ds[j, i], wq[i]) + nt(p[j, i], (rr[i] * c).astype(BF))
                acc = r if acc is None else acc + r
            dkp[j] = acc

    def pass_on(j, hf):
        lo, size = hf * (T // 2), T // 2
        total = dkp[j, pl.ds(lo, size), :]
        odd = j % 2 == 1
        if j < NZ - 3 or (j == NZ - 3 and hf == 0) or (j == NZ - 2 and hf == 1):
            arrive(drecv.at[j, pl.ds(lo, size)], dk_r.at[2 * j + hf])
            total = total + drecv[j, pl.ds(lo, size), :].astype(F32)
        dsend[j, pl.ds(lo, size), :] = total.astype(BF)
        if j == NZ - 1:
            onward = hf == 0
            to = max(NZ - 3, 0) if hf == 0 else max(NZ - 2, 1)
        else:
            onward = odd
            to = j - 2 if j >= 3 else (0 if j == 1 else NZ - 1)
        send(dsend.at[j, pl.ds(lo, size)], drecv.at[to, pl.ds(lo, size)], dk_s.at[2 * j + hf], dk_r.at[2 * to + hf],
             zdev(1 if onward else -1))

    def attended_rows():
        for i in range(1, NQ):
            arrive(orecv.at[i], o_r.at[i])
        orecv[0] = osend[0]
        own = Lg[pl.ds(qabs(0), 1), :]
        att = jnp.zeros((DH, T), F32)
        for s in range(NQ):
            att = att + jnp.exp(str_[s, pl.ds(qabs(0), 1), :] - own) * orecv[s].astype(F32)
        wgp = nn(att.astype(BF), gmb[...])
        for s in range(NQ):
            wg1s[s] = wgp[s * RW : (s + 1) * RW, :].astype(BF)
        for i in range(1, NQ):
            back = qback(i)
            send(wg1s.at[qabs(i)], wg1r.at[back], g1_s.at[i], g1_r.at[back], qdev(i))
        attall[mp] = (att * live_row).astype(BF)
        for r in range(1, NMP):
            send(attall.at[mp], attall.at[mp], at_s.at[r], at_r.at[r], mdev(r))

    def gradient_over_z():
        wg1r[0] = wg1s[qabs(0)]
        for i in range(1, NQ):
            arrive(wg1r.at[i], g1_r.at[i])
        part = wg1r[0].astype(F32)
        for i in range(1, NQ):
            part = part + wg1r[i].astype(F32)
        wg2[z] = part.astype(BF)
        for r in range(1, NZ):
            send(wg2.at[z], wg2.at[z], g2_s.at[r], g2_r.at[r], zdev(r))

    for n in range(H):
        key_pair(n)
        j = NB - 1 - 2 * n
        pass_on(j, 0)
        if n > 0:
            pass_on(j + 1, 1)
        pass_on(j, 1)
        if j > 1:
            pass_on(j - 1, 0)
        if n == max(H - 2, 0) and n > 0:
            gradient_over_z()
        if n == 0:
            attended_rows()
            for i in range(1, NQ):
                back = qback(i)
                send(dqsend.at[i], dqrecv.at[back], dq_s.at[i], dq_r.at[back], qdev(i))

    if H <= 2:
        gradient_over_z()

    for r in range(1, NMP):
        arrive(wall.at[0, 0], wl_r.at[r - 1])
        arrive(attall.at[0], at_r.at[r])
    att_rows = attall[...].reshape(NMP * DH, T).astype(F32).T.astype(BF)
    out_ref[...] = nn(att_rows, wall[...].reshape(NMP * DH, D)).astype(BF)

    total = dqacc[0]
    for i in range(1, NQ):
        arrive(dqrecv.at[i], dq_r.at[i])
        total = total + dqrecv[i].astype(F32)
    dq_ref[...] = total

    for hf in range(2):
        rows_of = pl.ds(hf * (T // 2), T // 2)
        total = dkp[0, rows_of, :]
        for slot in (0, NB - 1):
            if NZ > 2 or slot == hf:
                arrive(drecv.at[slot, rows_of], dk_r.at[2 * slot + hf])
                total = total + drecv[slot, rows_of, :].astype(F32)
        dkv_ref[rows_of, :] = total * live_col[hf * (T // 2) : (hf + 1) * (T // 2), :]

    for r in range(1, NZ):
        arrive(wg2.at[0], g2_r.at[r])
    part = wg2[0].astype(F32)
    for k in range(1, NZ):
        part = part + wg2[k].astype(F32)
    own = qabs(0)
    wg3[own] = part.astype(BF)
    for i in range(1, NQ):
        send(wg3.at[own], wg3.at[own], g3_s.at[i], g3_r.at[qback(i)], qdev(i))
    for i in range(1, NQ):
        arrive(wg3.at[0], g3_r.at[i])
    for s in range(NQ):
        wg_ref[s * RW : (s + 1) * RW, :] = wg3[s].astype(F32)

    for make in copies:
        src, ssem = make()
        rcopy(src, src, ssem, kv_r.at[0], partner).wait_send()


def WAITS(NB, H):
    return set(range(1, H - 1)) | {H // 2, NB - 1, max(NB - 5, 0), max(NB - 2, 0)}


def write_out(a_ref, b_ref, c_ref, d_ref, a_hbm, b_hbm, c_hbm, d_hbm, sem):
    pairs = ((a_ref, a_hbm), (b_ref, b_hbm), (c_ref, c_hbm), (d_ref, d_hbm))
    copies = [pltpu.make_async_copy(r, h, sem.at[n]) for n, (r, h) in enumerate(pairs)]
    for c in copies:
        c.start()
    for c in copies:
        c.wait()


def solution(mesh):
    NMP = mesh.shape["mp"]
    NSEQ = mesh.shape["seq"]
    NY, NZ = {64: (4, 8), 8: (2, 2), 16: (2, 4)}[NSEQ]
    NB, NQ = NZ, NY * CORES
    U = NQ // 2

    def shards(queries, key_value, tile_fill, out_weight, grad_output):
        T = queries.shape[0]
        D = out_weight.shape[2]
        qT = queries[:, 0, :].T
        kv = key_value[:, 0, :]
        w = out_weight.reshape(CORES, DH // CORES, out_weight.shape[2])
        V = pl.BlockSpec(memory_space=pltpu.VMEM)
        A = pl.BlockSpec(memory_space=pl.ANY)
        v = pltpu.VMEM
        dma = lambda n: pltpu.SemaphoreType.DMA((n,))
        RW = DH // NQ
        scratch = [
            pltpu.SMEM((T // TILE,), jnp.int32), v((DH, T), BF), v((T, 2 * DH), BF), v((T, D), BF), dma(5),
            v((NB, T + 16, 2 * DH), BF), v((NB, 2 * DH + 16, T), BF), v((NQ, DH, T), BF), v((NQ, DH, T), BF),
            v((NQ, 2 * DH, T), BF), v((NB, NQ, T, T), BF), v((NB, NQ, 8, T), F32), v((NQ, 8, T), F32),
            v((NQ, 2 * DH + 16, T), F32), v((2, U, 8, T), F32), v((NB, NQ, T, T), BF),
            v((U, T, T), F32), v((U, T, T), F32), v((NQ, 8, T), F32), v((NQ, 8, T), F32),
            v((NQ, 2 * DH, T), F32), v((NQ, 2 * DH, T), BF),
            v((2 * NQ, T), F32), v((NQ, 2 * NQ, T), F32), v((8, T), F32), v((8, T), F32),
            v((NQ, DH, T), BF), v((NQ, DH, T), BF), v((NB, T, 2 * DH), F32), v((NB, T, 2 * DH), BF), v((NB, T, 2 * DH), BF),
            v((NQ, DH, T), F32), v((NQ, DH, T), BF), v((NQ, DH, T), BF),
            v((T, D), BF), v((NMP, CORES, DH // CORES, D), BF), v((NMP, DH, T), BF),
            v((NQ, RW, D), BF), v((NQ, RW, D), BF), v((NZ, RW, D), BF), v((NQ, RW, D), BF),
            dma(4), dma(2 * NB), dma(2 * NB), dma(NQ), dma(NQ), dma(NQ), dma(NQ), dma(NQ), dma(NQ), dma(NQ), dma(NQ),
            dma(NQ), dma(NQ), dma(2 * NB), dma(2 * NB), dma(NQ), dma(NQ),
            dma(NMP), dma(NMP), dma(NMP), dma(NMP), dma(NMP), dma(NMP), dma(NQ), dma(NQ), dma(NZ), dma(NZ), dma(NQ), dma(NQ),
        ]
        shapes = [((T, D), BF), ((DH, T), F32), ((T, 2 * DH), F32), ((DH, D), F32)]
        results = pl.pallas_call(
            functools.partial(kernel, NY, NZ, NMP),
            name="voxel_attention",
            out_shape=[pltpu.VMEM(*s) for s in shapes],
            in_specs=[A, A, A, A, A],
            out_specs=[V, V, V, V],
            scratch_shapes=scratch,
            compiler_params=pltpu.CompilerParams(
                collective_id=0, has_side_effects=True, vmem_limit_bytes=56 * 1024 * 1024
            ),
        )(tile_fill, qT, kv, w, grad_output)
        out, dqT, dkv, wg = pl.pallas_call(
            write_out,
            name="write_out",
            out_shape=[jax.ShapeDtypeStruct(*s) for s in shapes],
            in_specs=[V, V, V, V],
            out_specs=[A, A, A, A],
            scratch_shapes=[dma(4)],
        )(*(pltpu.with_memory_space_constraint(r, pltpu.VMEM) for r in results))
        return out, dqT.T[:, None, :], dkv[:, None, :], wg[None]

    return jax.shard_map(
        shards,
        mesh=mesh,
        in_specs=(
            P("seq", "mp", None),
            P("seq", "mp", None),
            P("seq"),
            P("mp", None, None),
            P("seq", None),
        ),
        out_specs=(P("seq", None), P("seq", "mp", None), P("seq", "mp", None), P("mp", None, None)),
        check_vma=False,
    )
```

time: 75.4 us -> 66.6 us (0.88)
  Pallas kernels: 70.8 us -> 65.8 us
  local copies, waits for them, and re-layouts: 3.78 us -> 0 us
    pallas_call x1, Pallas kernels: 70.8 us -> 64.9 us  [shards(): pl.pallas_call(functools.partial(kernel, NY, NZ, NMP), name='voxel_attent...]
    unnamed x10 -> x0, local copies, waits for them, and re-layouts: 3.78 us -> none
    pallas_call x0 -> x1, Pallas kernels: none -> 0.91 us  [shards(): pl.pallas_call(write_out, name='write_out', out_shape=[jax.ShapeDtypeStru...]
where the time goes in v2:
time: 66.6 us; the launch traced here: 66.5 us
  Pallas kernels  65.8 us (99%)
    pallas_call x1, Pallas kernels, shards(): pl.pallas_call(functools.partial(kernel, NY, NZ, NMP), name='voxel_attent...  64.9 us

profile of v2, /device:TPU:1, one launch (start us, length us, event | category | flops | bytes accessed | tf_op | source)
XLA Modules:
  0.0 66.5 jit_solution(1455684927334828629)
XLA Ops:
  0.6 64.9 %voxel_attention.1 = (bf16[256,768]{1,0:T(8,128)(2,1)S(1)}, f32[64,256]{1,0:T(8,128)S(1)}, f32[256,128]{1,0:T(8,128)S(1)}, f32[64,768]{1,0:T(8,128)S(1)}) custom-call(s32[2]{0:T(128)} %fill_hbm.1, bf16[64,256]{1,0:T(8,128)(2,1)} %bitcast.14, bf16[256,128]{1,0:T(8,128)(2,1)} %bitcast.13, bf16[2,32,768]{2,1,0:T(8,128)(2,1)} %bitcast.12, bf16[256,768]{1,0:T(8,128)(2,1)} %g_hbm.1), custom_call_target="tpu_custom_call" | custom-call | tf_op jit(solution)/shard_map/voxel_attention/pallas_call | solution.py:569
  65.5 0.9 %write_out.1 = (bf16[256,768]{1,0:T(8,128)(2,1)}, f32[64,256]{1,0:T(8,128)}, f32[256,128]{1,0:T(8,128)}, f32[64,768]{1,0:T(8,128)}) custom-call(bf16[256,768]{1,0:T(8,128)(2,1)S(1)} %get-tuple-element.12.a_ref, f32[64,256]{1,0:T(8,128)S(1)} %get-tuple-element.13.b_ref, f32[256,128]{1,0:T(8,128)S(1)} %get-tuple-element.14.c_ref, ...), custom_call_target="tpu_custom_call" | custom-call | tf_op jit(solution)/shard_map/write_out/pallas_call | solution.py:580

commit v3 on v2

--- a/solution.py
+++ b/solution.py
@@ -42,7 +42,7 @@
     fill_ref, qT_ref, kv_ref, g_ref, in_sem,
     kvb, kvT, qq, dd, qS, p, mh, m, oacc, ab, ds,
     sA, sB, Ll, Dl, rr, wq,
-    stl, str_, Lg, Dg, osend, orecv, dkp, dsend, drecv, dqacc, dqsend, dqrecv,
+    stl, pst, str_, wpair, Lg, Dg, osend, opair, orecv, dkp, dsend, drecv, dqacc, dqsend, dqpair, dqrecv,
     gmb, wall, attall, wg1s, wg1r, wg2, wg3,
     kv0_s, kv_s, kv_r, q_s, q_r, ql_s, d_s, d_r, dl_s, st_s, st_r, o_s, o_r, dk_s, dk_r, dq_s, dq_r,
     w_s, w_r, wl_s, wl_r, at_s, at_r, g1_s, g1_r, g2_s, g2_r, g3_s, g3_r,
@@ -135,10 +135,6 @@
     kvb[0, T : T + 16, :] = tail.astype(BF)
     loads[1].wait()
     qq[0] = (qT_ref[...].astype(F32) * SCALE).astype(BF)
-    loads[2].wait()
-    loads[3].wait()
-    gmb[...] = (g_ref[...].astype(F32) * live_col).astype(BF)
-    dd[0] = nt(wall[mp].reshape(DH, D), gmb[...]).astype(BF)
 
     def prepare_keys(j):
         live16 = kvb[j, T : T + 16, :].astype(F32)
@@ -148,12 +144,6 @@
 
     def prepare_queries(i):
         qS[i, 0:DH, :] = qq[i]
-
-    prepare_keys(0)
-    prepare_queries(0)
-    for i in range(NQ):
-        qS[i, DH : 2 * DH, :] = jnp.zeros((DH, T), BF)
-        wq[i, DH : 2 * DH, :] = jnp.zeros((DH, T), BF)
 
     pl.semaphore_wait(barrier, (NB - 1) + (NQ - 1) + (NMP - 1))
 
@@ -190,9 +180,19 @@
         send(buf.at[0], buf.at[1], ssem.at[1], rsem.at[1], partner)
 
     spread(qq, q_s, q_r)
+    loads[2].wait()
+    loads[3].wait()
+    gmb[...] = (g_ref[...].astype(F32) * live_col).astype(BF)
+    dd[0] = nt(wall[mp].reshape(DH, D), gmb[...]).astype(BF)
     spread(dd, d_s, d_r)
     if YL == 2:
         send_row(wall, (mp, core), (mp, core), w_s, 0, w_r.at[0], (seq, head_at(1, 0)))
+    prepare_keys(0)
+    prepare_queries(0)
+    for i in range(NQ):
+        qS[i, DH : 2 * DH, :] = jnp.zeros((DH, T), BF)
+        wq[i, DH : 2 * DH, :] = jnp.zeros((DH, T), BF)
+
     for i in range(NQ):
         m[i] = jnp.full((8, T), -1e30, F32)
         oacc[i] = jnp.zeros((2 * DH + 16, T), F32)
@@ -317,7 +317,7 @@
         inv = 1.0 / total
         o = oacc[i, DH : 2 * DH, :] * inv
         oacc[i, 0:DH, :] = oacc[i, 0:DH, :] * inv
-        osend[i] = o.astype(BF)
+        osend[i % 2, i // 2] = o.astype(BF)
         lrow = m[i, 0:1, :] + jnp.log(total)
         drow = jnp.sum(o * dd[i].astype(F32), axis=0, keepdims=True)
         Ll[i, 0:1, :] = lrow
@@ -325,12 +325,31 @@
         stl[pl.ds(qabs(i), 1), :] = lrow
         stl[pl.ds(NQ + qabs(i), 1), :] = drow
 
-    for i in range(1, NQ):
-        back = qback(i)
-        send(stl, str_.at[back], st_s.at[i], st_r.at[back], qdev(i))
-    for i in range(1, NQ):
-        back = qback(i)
-        send(osend.at[i], orecv.at[back], o_s.at[i], o_r.at[back], qdev(i))
+    send(stl, pst, st_s.at[NY], st_r.at[NY], partner)
+    send(osend.at[1], opair, o_s.at[NY], o_r.at[NY], partner)
+
+    def chip_totals():
+        arrive(pst, st_r.at[NY])
+        la, lb = stl[0:NQ, :], pst[0:NQ, :]
+        top = jnp.maximum(la, lb)
+        wa, wb = jnp.exp(la - top), jnp.exp(lb - top)
+        both = wa + wb
+        inv = 1.0 / both
+        str_[0, 0:NQ, :] = top + jnp.log(both)
+        str_[0, NQ : 2 * NQ, :] = (wa * stl[NQ : 2 * NQ, :] + wb * pst[NQ : 2 * NQ, :]) * inv
+        for k in range(1, NY):
+            back = qback(2 * k) // 2
+            send(str_.at[0], str_.at[back], st_s.at[k], st_r.at[back], qdev(2 * k))
+        wpair[0] = wa * inv
+        wpair[1] = wb * inv
+        arrive(opair, o_r.at[NY])
+        for k in range(NY):
+            row = pl.ds(qabs(2 * k), 1)
+            mine = osend[0, k].astype(F32) * wpair[0, row, :]
+            osend[0, k] = (mine + opair[k].astype(F32) * wpair[1, row, :]).astype(BF)
+        for k in range(1, NY):
+            back = qback(2 * k) // 2
+            send(osend.at[0, k], orecv.at[back], o_s.at[k], o_r.at[back], qdev(2 * k))
 
     def Ust(j, half, buf):
         for t in range(U):
@@ -353,8 +372,7 @@
     Dst(0, 0, sA)
     Ust(0, 1, sB)
 
-    @pl.loop(1, NB)
-    def _(j):
+    def local_turn(j):
         Ust(j, 0, sA)
         Dst(j - 1, 1, sB)
         Mst(j - 1, 0)
@@ -362,13 +380,16 @@
         Dst(j, 0, sA)
         Mst(j - 1, 1)
 
+    cut = min(NB, 2)
+    pl.loop(1, cut)(local_turn)
+    chip_totals()
+    pl.loop(cut, NB)(local_turn)
     Dst(NB - 1, 1, sB)
     Mst(NB - 1, 0)
     Mst(NB - 1, 1)
 
-    str_[0] = stl[...]
-    for i in range(1, NQ):
-        arrive(str_.at[i], st_r.at[i])
+    for k in range(1, NY):
+        arrive(str_.at[k], st_r.at[k])
     if YL == 2:
         send_row(wall, (head_at(1, 0), core), (head_at(1, 0), core), wl_s, 0, wl_r.at[0], partner)
     for dx in range(1, X):
@@ -378,16 +399,33 @@
             arrive(wall.at[0, 0], w_r.at[k])
             send_row(wall, (h, core), (h, core), wl_s, k, wl_r.at[k], partner)
     big = str_[0, 0:NQ, :]
-    for s in range(1, NQ):
-        big = jnp.maximum(big, str_[s, 0:NQ, :])
+    for k in range(1, NY):
+        big = jnp.maximum(big, str_[k, 0:NQ, :])
     wsum = jnp.zeros((NQ, T), F32)
     dsum = jnp.zeros((NQ, T), F32)
-    for s in range(NQ):
-        wt = jnp.exp(str_[s, 0:NQ, :] - big)
+    for k in range(NY):
+        wt = jnp.exp(str_[k, 0:NQ, :] - big)
         wsum = wsum + wt
-        dsum = dsum + wt * str_[s, NQ : 2 * NQ, :]
+        dsum = dsum + wt * str_[k, NQ : 2 * NQ, :]
     Lg[0:NQ, :] = big + jnp.log(wsum)
     Dg[0:NQ, :] = dsum / wsum
+    def attended_rows():
+        own = pl.ds(qabs(0), 1)
+        att = jnp.exp(str_[0, own, :] - Lg[own, :]) * osend[0, 0].astype(F32)
+        for k in range(1, NY):
+            arrive(orecv.at[k], o_r.at[k])
+            att = att + jnp.exp(str_[k, own, :] - Lg[own, :]) * orecv[k].astype(F32)
+        wgp = nn(att.astype(BF), gmb[...])
+        for s in range(NQ):
+            wg1s[s] = wgp[s * RW : (s + 1) * RW, :].astype(BF)
+        for i in range(1, NQ):
+            back = qback(i)
+            send(wg1s.at[qabs(i)], wg1r.at[back], g1_s.at[i], g1_r.at[back], qdev(i))
+        attall[mp] = (att * live_row).astype(BF)
+        for r in range(1, NMP):
+            send(attall.at[mp], attall.at[mp], at_s.at[r], at_r.at[r], mdev(r))
+
+    attended_rows()
     for i in range(NQ):
         w = jnp.exp(Ll[i, 0:1, :] - Lg[pl.ds(qabs(i), 1), :])
         e = w * (Dl[i, 0:1, :] - Dg[pl.ds(qabs(i), 1), :])
@@ -399,7 +437,10 @@
         if i == 0:
             dqacc[0] = total
         else:
-            dqsend[i] = total.astype(BF)
+            dqacc[i] = total
+            if i % 2 == 1:
+                dqsend[1, i // 2] = total.astype(BF)
+    send(dqsend.at[1], dqpair, dq_s.at[NY], dq_r.at[NY], partner)
 
     def key_pair(n):
         @pl.loop(0, 2)
@@ -429,24 +470,6 @@
         send(dsend.at[j, pl.ds(lo, size)], drecv.at[to, pl.ds(lo, size)], dk_s.at[2 * j + hf], dk_r.at[2 * to + hf],
              zdev(1 if onward else -1))
 
-    def attended_rows():
-        for i in range(1, NQ):
-            arrive(orecv.at[i], o_r.at[i])
-        orecv[0] = osend[0]
-        own = Lg[pl.ds(qabs(0), 1), :]
-        att = jnp.zeros((DH, T), F32)
-        for s in range(NQ):
-            att = att + jnp.exp(str_[s, pl.ds(qabs(0), 1), :] - own) * orecv[s].astype(F32)
-        wgp = nn(att.astype(BF), gmb[...])
-        for s in range(NQ):
-            wg1s[s] = wgp[s * RW : (s + 1) * RW, :].astype(BF)
-        for i in range(1, NQ):
-            back = qback(i)
-            send(wg1s.at[qabs(i)], wg1r.at[back], g1_s.at[i], g1_r.at[back], qdev(i))
-        attall[mp] = (att * live_row).astype(BF)
-        for r in range(1, NMP):
-            send(attall.at[mp], attall.at[mp], at_s.at[r], at_r.at[r], mdev(r))
-
     def gradient_over_z():
         wg1r[0] = wg1s[qabs(0)]
         for i in range(1, NQ):
@@ -460,6 +483,8 @@
 
     for n in range(H):
         key_pair(n)
+        if n == H - 2 and n > 0:
+            gradient_over_z()
         j = NB - 1 - 2 * n
         pass_on(j, 0)
         if n > 0:
@@ -467,37 +492,15 @@
         pass_on(j, 1)
         if j > 1:
             pass_on(j - 1, 0)
-        if n == max(H - 2, 0) and n > 0:
-            gradient_over_z()
         if n == 0:
-            attended_rows()
-            for i in range(1, NQ):
-                back = qback(i)
-                send(dqsend.at[i], dqrecv.at[back], dq_s.at[i], dq_r.at[back], qdev(i))
-
+            arrive(dqpair, dq_r.at[NY])
+            dqacc[0] += dqpair[0].astype(F32)
+            for k in range(1, NY):
+                dqsend[0, k] = (dqacc[2 * k] + dqpair[k].astype(F32)).astype(BF)
+                back = qback(2 * k) // 2
+                send(dqsend.at[0, k], dqrecv.at[back], dq_s.at[k], dq_r.at[back], qdev(2 * k))
     if H <= 2:
         gradient_over_z()
-
-    for r in range(1, NMP):
-        arrive(wall.at[0, 0], wl_r.at[r - 1])
-        arrive(attall.at[0], at_r.at[r])
-    att_rows = attall[...].reshape(NMP * DH, T).astype(F32).T.astype(BF)
-    out_ref[...] = nn(att_rows, wall[...].reshape(NMP * DH, D)).astype(BF)
-
-    total = dqacc[0]
-    for i in range(1, NQ):
-        arrive(dqrecv.at[i], dq_r.at[i])
-        total = total + dqrecv[i].astype(F32)
-    dq_ref[...] = total
-
-    for hf in range(2):
-        rows_of = pl.ds(hf * (T // 2), T // 2)
-        total = dkp[0, rows_of, :]
-        for slot in (0, NB - 1):
-            if NZ > 2 or slot == hf:
-                arrive(drecv.at[slot, rows_of], dk_r.at[2 * slot + hf])
-                total = total + drecv[slot, rows_of, :].astype(F32)
-        dkv_ref[rows_of, :] = total * live_col[hf * (T // 2) : (hf + 1) * (T // 2), :]
 
     for r in range(1, NZ):
         arrive(wg2.at[0], g2_r.at[r])
@@ -508,6 +511,28 @@
     wg3[own] = part.astype(BF)
     for i in range(1, NQ):
         send(wg3.at[own], wg3.at[own], g3_s.at[i], g3_r.at[qback(i)], qdev(i))
+
+    for r in range(1, NMP):
+        arrive(wall.at[0, 0], wl_r.at[r - 1])
+        arrive(attall.at[0], at_r.at[r])
+    att_rows = attall[...].reshape(NMP * DH, T).astype(F32).T.astype(BF)
+    out_ref[...] = nn(att_rows, wall[...].reshape(NMP * DH, D)).astype(BF)
+
+    total = dqacc[0]
+    for k in range(1, NY):
+        arrive(dqrecv.at[k], dq_r.at[k])
+        total = total + dqrecv[k].astype(F32)
+    dq_ref[...] = total
+
+    for hf in range(2):
+        rows_of = pl.ds(hf * (T // 2), T // 2)
+        total = dkp[0, rows_of, :]
+        for slot in (0, NB - 1):
+            if NZ > 2 or slot == hf:
+                arrive(drecv.at[slot, rows_of], dk_r.at[2 * slot + hf])
+                total = total + drecv[slot, rows_of, :].astype(F32)
+        dkv_ref[rows_of, :] = total * live_col[hf * (T // 2) : (hf + 1) * (T // 2), :]
+
     for i in range(1, NQ):
         arrive(wg3.at[0], g3_r.at[i])
     for s in range(NQ):
@@ -556,9 +581,9 @@
             v((NQ, 2 * DH + 16, T), F32), v((2, U, 8, T), F32), v((NB, NQ, T, T), BF),
             v((U, T, T), F32), v((U, T, T), F32), v((NQ, 8, T), F32), v((NQ, 8, T), F32),
             v((NQ, 2 * DH, T), F32), v((NQ, 2 * DH, T), BF),
-            v((2 * NQ, T), F32), v((NQ, 2 * NQ, T), F32), v((8, T), F32), v((8, T), F32),
-            v((NQ, DH, T), BF), v((NQ, DH, T), BF), v((NB, T, 2 * DH), F32), v((NB, T, 2 * DH), BF), v((NB, T, 2 * DH), BF),
-            v((NQ, DH, T), F32), v((NQ, DH, T), BF), v((NQ, DH, T), BF),
+            v((2 * NQ, T), F32), v((2 * NQ, T), F32), v((NY, 2 * NQ, T), F32), v((2, NQ, T), F32), v((8, T), F32), v((8, T), F32),
+            v((2, NY, DH, T), BF), v((NY, DH, T), BF), v((NY, DH, T), BF), v((NB, T, 2 * DH), F32), v((NB, T, 2 * DH), BF), v((NB, T, 2 * DH), BF),
+            v((NQ, DH, T), F32), v((2, NY, DH, T), BF), v((NY, DH, T), BF), v((NY, DH, T), BF),
             v((T, D), BF), v((NMP, CORES, DH // CORES, D), BF), v((NMP, DH, T), BF),
             v((NQ, RW, D), BF), v((NQ, RW, D), BF), v((NZ, RW, D), BF), v((NQ, RW, D), BF),
             dma(4), dma(2 * NB), dma(2 * NB), dma(NQ), dma(NQ), dma(NQ), dma(NQ), dma(NQ), dma(NQ), dma(NQ), dma(NQ),

time: 66.6 us -> 63.1 us (0.947)
  Pallas kernels: 65.8 us -> 62.2 us
    pallas_call x1, Pallas kernels: 64.9 us -> 61.2 us  [shards(): pl.pallas_call(functools.partial(kernel, NY, NZ, NMP), name='voxel_attent...]
where the time goes in v3:
time: 63.1 us; the launch traced here: 62.8 us
  Pallas kernels  62.2 us (99%)
  between operations  0.64 us (1%)
    pallas_call x1, Pallas kernels, shards(): pl.pallas_call(functools.partial(kernel, NY, NZ, NMP), name='voxel_attent...  61.2 us

profile of v3, /device:TPU:1, one launch (start us, length us, event | category | flops | bytes accessed | tf_op | source)
XLA Modules:
  0.0 62.8 jit_solution(10361503020109113473)
XLA Ops:
  0.6 61.2 %voxel_attention.1 = (bf16[256,768]{1,0:T(8,128)(2,1)S(1)}, f32[64,256]{1,0:T(8,128)S(1)}, f32[256,128]{1,0:T(8,128)S(1)}, f32[64,768]{1,0:T(8,128)S(1)}) custom-call(s32[2]{0:T(128)} %fill_hbm.1, bf16[64,256]{1,0:T(8,128)(2,1)} %bitcast.14, bf16[256,128]{1,0:T(8,128)(2,1)} %bitcast.13, bf16[2,32,768]{2,1,0:T(8,128)(2,1)} %bitcast.12, bf16[256,768]{1,0:T(8,128)(2,1)} %g_hbm.1), custom_call_target="tpu_custom_call" | custom-call | tf_op jit(solution)/shard_map/voxel_attention/pallas_call | solution.py:594
  61.9 0.9 %write_out.1 = (bf16[256,768]{1,0:T(8,128)(2,1)}, f32[64,256]{1,0:T(8,128)}, f32[256,128]{1,0:T(8,128)}, f32[64,768]{1,0:T(8,128)}) custom-call(bf16[256,768]{1,0:T(8,128)(2,1)S(1)} %get-tuple-element.12.a_ref, f32[64,256]{1,0:T(8,128)S(1)} %get-tuple-element.13.b_ref, f32[256,128]{1,0:T(8,128)S(1)} %get-tuple-element.14.c_ref, ...), custom_call_target="tpu_custom_call" | custom-call | tf_op jit(solution)/shard_map/write_out/pallas_call | solution.py:605

commit v4 on v3

--- a/solution.py
+++ b/solution.py
@@ -44,7 +44,7 @@
     sA, sB, Ll, Dl, rr, wq,
     stl, pst, str_, wpair, Lg, Dg, osend, opair, orecv, dkp, dsend, drecv, dqacc, dqsend, dqpair, dqrecv,
     gmb, wall, attall, wg1s, wg1r, wg2, wg3,
-    kv0_s, kv_s, kv_r, q_s, q_r, ql_s, d_s, d_r, dl_s, st_s, st_r, o_s, o_r, dk_s, dk_r, dq_s, dq_r,
+    kv0_s, kv_s, kv_r, qf_s, qf_r, q_s, q_r, ql_s, d_s, d_r, dl_s, st_s, st_r, o_s, o_r, dk_s, dk_r, dq_s, dq_r,
     w_s, w_r, wl_s, wl_r, at_s, at_r, g1_s, g1_r, g2_s, g2_r, g3_s, g3_r,
 ):
     T = kv_ref.shape[0]
@@ -96,12 +96,11 @@
         )
 
     barrier = pltpu.get_barrier_semaphore()
-    for j in range(1, NB):
-        pl.semaphore_signal(barrier, inc=1, device_id=zdev(offset_of(j)), device_id_type=MESH)
-    for i in range(1, NQ):
-        pl.semaphore_signal(barrier, inc=1, device_id=qdev(i), device_id_type=MESH)
-    for r in range(1, NMP):
-        pl.semaphore_signal(barrier, inc=1, device_id=mdev(r), device_id_type=MESH)
+    near = [zdev(offset_of(j)) for j in range(1, min(NB, 3))] + [partner]
+    near += [qdev(2 * k) for k in range(1, min(NY, 3))]
+    near += [(seq, head_at(1, 0))] * (YL - 1) + [(seq, head_at(0, dx)) for dx in range(1, X)]
+    for dev in near:
+        pl.semaphore_signal(barrier, inc=1, device_id=dev, device_id_type=MESH)
 
     w_ref = wall.at[mp]
     loads = [
@@ -145,7 +144,7 @@
     def prepare_queries(i):
         qS[i, 0:DH, :] = qq[i]
 
-    pl.semaphore_wait(barrier, (NB - 1) + (NQ - 1) + (NMP - 1))
+    pl.semaphore_wait(barrier, len(near))
 
     copies = []
 
@@ -174,7 +173,7 @@
             send_keys(0, hf, 1, kv0_s, 2 + hf, zdev(-1))
 
     def spread(buf, ssem, rsem):
-        for k in range(1, NY):
+        for k in range(1, min(NY, 3)):
             i, back = 2 * k, qback(2 * k)
             send(buf.at[0], buf.at[back], ssem.at[i], rsem.at[back], qdev(i))
         send(buf.at[0], buf.at[1], ssem.at[1], rsem.at[1], partner)
@@ -226,22 +225,26 @@
             js = [NB - 1]
         take(js)
         if it == 0:
-            for k in range(1, max(NY - 1, 1)):
+            for k in range(1, min(NY, 3)):
                 relay(qq, ql_s, q_r, k)
+                if NY == 4:
+                    cut = pl.ds((k - 1) * (DH // 2), DH // 2)
+                    send(qq.at[2 * k, cut], qq.at[6, cut], qf_s.at[k - 1], qf_r.at[k - 1], qdev(6 - 2 * k))
+            if H > 2:
+                take([3, 4])
+                js = js + [3, 4]
+            if NY == 4:
+                for k in range(1, 3):
+                    arrive(qq.at[6, pl.ds((k - 1) * (DH // 2), DH // 2)], qf_r.at[k - 1])
+                send(qq.at[6], qq.at[7], ql_s.at[6], q_r.at[7], partner)
+                send(dd.at[0], dd.at[6], d_s.at[6], d_r.at[6], qdev(6))
         for half in range(2):
             if it == half * (H // 2):
-                if half == 1 and it == 0:
-                    relay(qq, ql_s, q_r, NY - 1)
                 for i in range(half * U, half * U + U):
                     if i % 2 == 1:
                         arrive(qq.at[i], q_r.at[i])
                     if i > 0:
                         prepare_queries(i)
-        if it == 0 and H > 2:
-            take([3, 4])
-            js = js + [3, 4]
-        if it == 0 and H // 2 > 0:
-            relay(qq, ql_s, q_r, NY - 1)
         for j in js:
             prepare_keys(j)
         if it == max(NB - 5, 0):
@@ -425,7 +428,6 @@
         for r in range(1, NMP):
             send(attall.at[mp], attall.at[mp], at_s.at[r], at_r.at[r], mdev(r))
 
-    attended_rows()
     for i in range(NQ):
         w = jnp.exp(Ll[i, 0:1, :] - Lg[pl.ds(qabs(i), 1), :])
         e = w * (Dl[i, 0:1, :] - Dg[pl.ds(qabs(i), 1), :])
@@ -483,8 +485,6 @@
 
     for n in range(H):
         key_pair(n)
-        if n == H - 2 and n > 0:
-            gradient_over_z()
         j = NB - 1 - 2 * n
         pass_on(j, 0)
         if n > 0:
@@ -492,7 +492,10 @@
         pass_on(j, 1)
         if j > 1:
             pass_on(j - 1, 0)
+        if n == H - 2 and n > 0:
+            gradient_over_z()
         if n == 0:
+            attended_rows()
             arrive(dqpair, dq_r.at[NY])
             dqacc[0] += dqpair[0].astype(F32)
             for k in range(1, NY):
@@ -501,6 +504,12 @@
                 send(dqsend.at[0, k], dqrecv.at[back], dq_s.at[k], dq_r.at[back], qdev(2 * k))
     if H <= 2:
         gradient_over_z()
+
+    for r in range(1, NMP):
+        arrive(wall.at[0, 0], wl_r.at[r - 1])
+        arrive(attall.at[0], at_r.at[r])
+    att_rows = attall[...].reshape(NMP * DH, T).astype(F32).T.astype(BF)
+    out_ref[...] = nn(att_rows, wall[...].reshape(NMP * DH, D)).astype(BF)
 
     for r in range(1, NZ):
         arrive(wg2.at[0], g2_r.at[r])
@@ -511,12 +520,6 @@
     wg3[own] = part.astype(BF)
     for i in range(1, NQ):
         send(wg3.at[own], wg3.at[own], g3_s.at[i], g3_r.at[qback(i)], qdev(i))
-
-    for r in range(1, NMP):
-        arrive(wall.at[0, 0], wl_r.at[r - 1])
-        arrive(attall.at[0], at_r.at[r])
-    att_rows = attall[...].reshape(NMP * DH, T).astype(F32).T.astype(BF)
-    out_ref[...] = nn(att_rows, wall[...].reshape(NMP * DH, D)).astype(BF)
 
     total = dqacc[0]
     for k in range(1, NY):
@@ -586,7 +589,7 @@
             v((NQ, DH, T), F32), v((2, NY, DH, T), BF), v((NY, DH, T), BF), v((NY, DH, T), BF),
             v((T, D), BF), v((NMP, CORES, DH // CORES, D), BF), v((NMP, DH, T), BF),
             v((NQ, RW, D), BF), v((NQ, RW, D), BF), v((NZ, RW, D), BF), v((NQ, RW, D), BF),
-            dma(4), dma(2 * NB), dma(2 * NB), dma(NQ), dma(NQ), dma(NQ), dma(NQ), dma(NQ), dma(NQ), dma(NQ), dma(NQ),
+            dma(4), dma(2 * NB), dma(2 * NB), dma(2), dma(2), dma(NQ), dma(NQ), dma(NQ), dma(NQ), dma(NQ), dma(NQ), dma(NQ), dma(NQ),
             dma(NQ), dma(NQ), dma(2 * NB), dma(2 * NB), dma(NQ), dma(NQ),
             dma(NMP), dma(NMP), dma(NMP), dma(NMP), dma(NMP), dma(NMP), dma(NQ), dma(NQ), dma(NZ), dma(NZ), dma(NQ), dma(NQ),
         ]

time: 63.1 us -> 62 us (0.983)
  Pallas kernels: 62.2 us -> 61.3 us
    pallas_call x1, Pallas kernels: 61.2 us -> 60.4 us  [shards(): pl.pallas_call(functools.partial(kernel, NY, NZ, NMP), name='voxel_attent...]
where the time goes in v4:
time: 62 us; the launch traced here: 61.9 us
  Pallas kernels  61.3 us (99%)
  between operations  0.64 us (1%)
    pallas_call x1, Pallas kernels, shards(): pl.pallas_call(functools.partial(kernel, NY, NZ, NMP), name='voxel_attent...  60.4 us

profile of v4, /device:TPU:1, one launch (start us, length us, event | category | flops | bytes accessed | tf_op | source)
XLA Modules:
  0.0 61.9 jit_solution(6322965146705491287)
XLA Ops:
  0.6 60.4 %voxel_attention.1 = (bf16[256,768]{1,0:T(8,128)(2,1)S(1)}, f32[64,256]{1,0:T(8,128)S(1)}, f32[256,128]{1,0:T(8,128)S(1)}, f32[64,768]{1,0:T(8,128)S(1)}) custom-call(s32[2]{0:T(128)} %fill_hbm.1, bf16[64,256]{1,0:T(8,128)(2,1)} %bitcast.14, bf16[256,128]{1,0:T(8,128)(2,1)} %bitcast.13, bf16[2,32,768]{2,1,0:T(8,128)(2,1)} %bitcast.12, bf16[256,768]{1,0:T(8,128)(2,1)} %g_hbm.1), custom_call_target="tpu_custom_call" | custom-call | tf_op jit(solution)/shard_map/voxel_attention/pallas_call | solution.py:597
  61.0 0.9 %write_out.1 = (bf16[256,768]{1,0:T(8,128)(2,1)}, f32[64,256]{1,0:T(8,128)}, f32[256,128]{1,0:T(8,128)}, f32[64,768]{1,0:T(8,128)}) custom-call(bf16[256,768]{1,0:T(8,128)(2,1)S(1)} %get-tuple-element.12.a_ref, f32[64,256]{1,0:T(8,128)S(1)} %get-tuple-element.13.b_ref, f32[256,128]{1,0:T(8,128)S(1)} %get-tuple-element.14.c_ref, ...), custom_call_target="tpu_custom_call" | custom-call | tf_op jit(solution)/shard_map/write_out/pallas_call | solution.py:608

commit v5 on v4

--- a/solution.py
+++ b/solution.py
@@ -44,7 +44,7 @@
     sA, sB, Ll, Dl, rr, wq,
     stl, pst, str_, wpair, Lg, Dg, osend, opair, orecv, dkp, dsend, drecv, dqacc, dqsend, dqpair, dqrecv,
     gmb, wall, attall, wg1s, wg1r, wg2, wg3,
-    kv0_s, kv_s, kv_r, qf_s, qf_r, q_s, q_r, ql_s, d_s, d_r, dl_s, st_s, st_r, o_s, o_r, dk_s, dk_r, dq_s, dq_r,
+    kv0_s, kv_s, kv_r, qf_s, qf_r, df_s, df_r, q_s, q_r, ql_s, d_s, d_r, dl_s, st_s, st_r, o_s, o_r, dk_s, dk_r, dq_s, dq_r,
     w_s, w_r, wl_s, wl_r, at_s, at_r, g1_s, g1_r, g2_s, g2_r, g3_s, g3_r,
 ):
     T = kv_ref.shape[0]
@@ -202,6 +202,14 @@
         arrive(buf.at[i], rsem.at[i])
         send_row(buf, i, i + 1, lsem, i, rsem.at[i + 1], partner)
 
+    def half_of(k):
+        return pl.ds((k - 1) * (DH // 2), DH // 2)
+
+    def send_half(buf, k, ssem, rsem):
+        src, dst = buf.at[2 * k, half_of(k)], buf.at[6, half_of(k)]
+        rcopy(src, dst, ssem.at[k - 1], rsem.at[k - 1], qdev(6 - 2 * k)).start()
+        copies.append(lambda: (buf.at[0, half_of(k)], ssem.at[k - 1]))
+
     def forward_keys(j, hf):
         arrive(kvb.at[j, pl.ds(*CUTS[hf])], kv_r.at[2 * j + hf])
         k = (j + 1) // 2
@@ -228,16 +236,14 @@
             for k in range(1, min(NY, 3)):
                 relay(qq, ql_s, q_r, k)
                 if NY == 4:
-                    cut = pl.ds((k - 1) * (DH // 2), DH // 2)
-                    send(qq.at[2 * k, cut], qq.at[6, cut], qf_s.at[k - 1], qf_r.at[k - 1], qdev(6 - 2 * k))
+                    send_half(qq, k, qf_s, qf_r)
             if H > 2:
                 take([3, 4])
                 js = js + [3, 4]
-            if NY == 4:
-                for k in range(1, 3):
-                    arrive(qq.at[6, pl.ds((k - 1) * (DH // 2), DH // 2)], qf_r.at[k - 1])
-                send(qq.at[6], qq.at[7], ql_s.at[6], q_r.at[7], partner)
-                send(dd.at[0], dd.at[6], d_s.at[6], d_r.at[6], qdev(6))
+        if it == min(1, H // 2) and NY == 4:
+            for k in range(1, 3):
+                arrive(qq.at[6, half_of(k)], qf_r.at[k - 1])
+            send_row(qq, 6, 7, ql_s, 6, q_r.at[7], partner)
         for half in range(2):
             if it == half * (H // 2):
                 for i in range(half * U, half * U + U):
@@ -255,9 +261,15 @@
                     k = 1 + 2 * (dx - 1) + flip
                     h = head_at(flip, 0)
                     send_row(wall, (h, core), (h, core), w_s, k, w_r.at[k], (seq, head_at(0, dx)))
-        if it == max(NB - 2, 0):
-            for k in range(1, NY):
+        if it == 1:
+            for k in range(1, min(NY, 3)):
                 relay(dd, dl_s, d_r, k)
+                if NY == 4:
+                    send_half(dd, k, df_s, df_r)
+        if it == max(NB - 2, 1) and NY == 4:
+            for k in range(1, 3):
+                arrive(dd.at[6, half_of(k)], df_r.at[k - 1])
+            send_row(dd, 6, 7, dl_s, 6, d_r.at[7], partner)
 
     def step_of(n):
         late = n - 2 * H
@@ -329,7 +341,8 @@
         stl[pl.ds(NQ + qabs(i), 1), :] = drow
 
     send(stl, pst, st_s.at[NY], st_r.at[NY], partner)
-    send(osend.at[1], opair, o_s.at[NY], o_r.at[NY], partner)
+    for k in reversed(range(NY)):
+        send(osend.at[1, k], opair.at[k], o_s.at[NY + k], o_r.at[NY + k], partner)
 
     def chip_totals():
         arrive(pst, st_r.at[NY])
@@ -345,14 +358,14 @@
             send(str_.at[0], str_.at[back], st_s.at[k], st_r.at[back], qdev(2 * k))
         wpair[0] = wa * inv
         wpair[1] = wb * inv
-        arrive(opair, o_r.at[NY])
-        for k in range(NY):
+        for k in reversed(range(NY)):
+            arrive(opair.at[k], o_r.at[NY + k])
             row = pl.ds(qabs(2 * k), 1)
             mine = osend[0, k].astype(F32) * wpair[0, row, :]
             osend[0, k] = (mine + opair[k].astype(F32) * wpair[1, row, :]).astype(BF)
-        for k in range(1, NY):
-            back = qback(2 * k) // 2
-            send(osend.at[0, k], orecv.at[back], o_s.at[k], o_r.at[back], qdev(2 * k))
+            if k > 0:
+                back = qback(2 * k) // 2
+                send(osend.at[0, k], orecv.at[back], o_s.at[k], o_r.at[back], qdev(2 * k))
 
     def Ust(j, half, buf):
         for t in range(U):
@@ -364,7 +377,7 @@
     def Dst(j, half, buf):
         for t in range(U):
             i = half * U + t
-            ds[j, i] = (p[j, i].astype(F32) * buf[t]).astype(BF)
+            ds[j, i] = p[j, i] * buf[t].astype(BF)
 
     def Mst(j, half):
         for t in range(U):
@@ -393,14 +406,6 @@
 
     for k in range(1, NY):
         arrive(str_.at[k], st_r.at[k])
-    if YL == 2:
-        send_row(wall, (head_at(1, 0), core), (head_at(1, 0), core), wl_s, 0, wl_r.at[0], partner)
-    for dx in range(1, X):
-        for flip in range(YL):
-            k = 1 + 2 * (dx - 1) + flip
-            h = head_at(flip, -dx)
-            arrive(wall.at[0, 0], w_r.at[k])
-            send_row(wall, (h, core), (h, core), wl_s, k, wl_r.at[k], partner)
     big = str_[0, 0:NQ, :]
     for k in range(1, NY):
         big = jnp.maximum(big, str_[k, 0:NQ, :])
@@ -425,6 +430,9 @@
             back = qback(i)
             send(wg1s.at[qabs(i)], wg1r.at[back], g1_s.at[i], g1_r.at[back], qdev(i))
         attall[mp] = (att * live_row).astype(BF)
+        for dx in range(1, X):
+            for flip in range(YL):
+                arrive(wall.at[0, 0], w_r.at[1 + 2 * (dx - 1) + flip])
         for r in range(1, NMP):
             send(attall.at[mp], attall.at[mp], at_s.at[r], at_r.at[r], mdev(r))
 
@@ -442,7 +450,6 @@
             dqacc[i] = total
             if i % 2 == 1:
                 dqsend[1, i // 2] = total.astype(BF)
-    send(dqsend.at[1], dqpair, dq_s.at[NY], dq_r.at[NY], partner)
 
     def key_pair(n):
         @pl.loop(0, 2)
@@ -483,8 +490,25 @@
         for r in range(1, NZ):
             send(wg2.at[z], wg2.at[z], g2_s.at[r], g2_r.at[r], zdev(r))
 
+    def less_urgent():
+        arrive(dqpair, dq_r.at[NY])
+        dqacc[0] += dqpair[0].astype(F32)
+        for k in range(1, NY):
+            dqsend[0, k] = (dqacc[2 * k] + dqpair[k].astype(F32)).astype(BF)
+            back = qback(2 * k) // 2
+            send(dqsend.at[0, k], dqrecv.at[back], dq_s.at[k], dq_r.at[back], qdev(2 * k))
+        if YL == 2:
+            send_row(wall, (head_at(1, 0), core), (head_at(1, 0), core), wl_s, 0, wl_r.at[0], partner)
+        for dx in range(1, X):
+            for flip in range(YL):
+                k = 1 + 2 * (dx - 1) + flip
+                h = head_at(flip, -dx)
+                send_row(wall, (h, core), (h, core), wl_s, k, wl_r.at[k], partner)
+
     for n in range(H):
         key_pair(n)
+        if n == H - 2 and n > 0:
+            gradient_over_z()
         j = NB - 1 - 2 * n
         pass_on(j, 0)
         if n > 0:
@@ -492,24 +516,13 @@
         pass_on(j, 1)
         if j > 1:
             pass_on(j - 1, 0)
-        if n == H - 2 and n > 0:
-            gradient_over_z()
         if n == 0:
             attended_rows()
-            arrive(dqpair, dq_r.at[NY])
-            dqacc[0] += dqpair[0].astype(F32)
-            for k in range(1, NY):
-                dqsend[0, k] = (dqacc[2 * k] + dqpair[k].astype(F32)).astype(BF)
-                back = qback(2 * k) // 2
-                send(dqsend.at[0, k], dqrecv.at[back], dq_s.at[k], dq_r.at[back], qdev(2 * k))
+            send(dqsend.at[1], dqpair, dq_s.at[NY], dq_r.at[NY], partner)
+        if n == min(1, H - 1):
+            less_urgent()
     if H <= 2:
         gradient_over_z()
-
-    for r in range(1, NMP):
-        arrive(wall.at[0, 0], wl_r.at[r - 1])
-        arrive(attall.at[0], at_r.at[r])
-    att_rows = attall[...].reshape(NMP * DH, T).astype(F32).T.astype(BF)
-    out_ref[...] = nn(att_rows, wall[...].reshape(NMP * DH, D)).astype(BF)
 
     for r in range(1, NZ):
         arrive(wg2.at[0], g2_r.at[r])
@@ -521,6 +534,12 @@
     for i in range(1, NQ):
         send(wg3.at[own], wg3.at[own], g3_s.at[i], g3_r.at[qback(i)], qdev(i))
 
+    for r in range(1, NMP):
+        arrive(wall.at[0, 0], wl_r.at[r - 1])
+        arrive(attall.at[0], at_r.at[r])
+    att_rows = attall[...].reshape(NMP * DH, T).astype(F32).T.astype(BF)
+    out_ref[...] = nn(att_rows, wall[...].reshape(NMP * DH, D)).astype(BF)
+
     total = dqacc[0]
     for k in range(1, NY):
         arrive(dqrecv.at[k], dq_r.at[k])
@@ -547,7 +566,7 @@
 
 
 def WAITS(NB, H):
-    return set(range(1, H - 1)) | {H // 2, NB - 1, max(NB - 5, 0), max(NB - 2, 0)}
+    return set(range(1, H - 1)) | {1} | {H // 2, NB - 1, max(NB - 5, 0), max(NB - 2, 0)}
 
 
 def write_out(a_ref, b_ref, c_ref, d_ref, a_hbm, b_hbm, c_hbm, d_hbm, sem):
@@ -589,7 +608,7 @@
             v((NQ, DH, T), F32), v((2, NY, DH, T), BF), v((NY, DH, T), BF), v((NY, DH, T), BF),
             v((T, D), BF), v((NMP, CORES, DH // CORES, D), BF), v((NMP, DH, T), BF),
             v((NQ, RW, D), BF), v((NQ, RW, D), BF), v((NZ, RW, D), BF), v((NQ, RW, D), BF),
-            dma(4), dma(2 * NB), dma(2 * NB), dma(2), dma(2), dma(NQ), dma(NQ), dma(NQ), dma(NQ), dma(NQ), dma(NQ), dma(NQ), dma(NQ),
+            dma(4), dma(2 * NB), dma(2 * NB), dma(2), dma(2), dma(2), dma(2), dma(NQ), dma(NQ), dma(NQ), dma(NQ), dma(NQ), dma(NQ), dma(NQ), dma(NQ),
             dma(NQ), dma(NQ), dma(2 * NB), dma(2 * NB), dma(NQ), dma(NQ),
             dma(NMP), dma(NMP), dma(NMP), dma(NMP), dma(NMP), dma(NMP), dma(NQ), dma(NQ), dma(NZ), dma(NZ), dma(NQ), dma(NQ),
         ]

time: 62 us -> 62 us (level)
  no operation moved by 1% of the time
where the time goes in v5:
time: 62 us; the launch traced here: 61.9 us
  Pallas kernels  61.3 us (99%)
  between operations  0.64 us (1%)
    pallas_call x1, Pallas kernels, shards(): pl.pallas_call(functools.partial(kernel, NY, NZ, NMP), name='voxel_attent...  60.4 us

profile of v5, /device:TPU:1, one launch (start us, length us, event | category | flops | bytes accessed | tf_op | source)
XLA Modules:
  0.0 61.9 jit_solution(12452293704601968799)
XLA Ops:
  0.6 60.4 %voxel_attention.1 = (bf16[256,768]{1,0:T(8,128)(2,1)S(1)}, f32[64,256]{1,0:T(8,128)S(1)}, f32[256,128]{1,0:T(8,128)S(1)}, f32[64,768]{1,0:T(8,128)S(1)}) custom-call(s32[2]{0:T(128)} %fill_hbm.1, bf16[64,256]{1,0:T(8,128)(2,1)} %bitcast.14, bf16[256,128]{1,0:T(8,128)(2,1)} %bitcast.13, bf16[2,32,768]{2,1,0:T(8,128)(2,1)} %bitcast.12, bf16[256,768]{1,0:T(8,128)(2,1)} %g_hbm.1), custom_call_target="tpu_custom_call" | custom-call | tf_op jit(solution)/shard_map/voxel_attention/pallas_call | solution.py:616
  61.0 0.9 %write_out.1 = (bf16[256,768]{1,0:T(8,128)(2,1)}, f32[64,256]{1,0:T(8,128)}, f32[256,128]{1,0:T(8,128)}, f32[64,768]{1,0:T(8,128)}) custom-call(bf16[256,768]{1,0:T(8,128)(2,1)S(1)} %get-tuple-element.12.a_ref, f32[64,256]{1,0:T(8,128)S(1)} %get-tuple-element.13.b_ref, f32[256,128]{1,0:T(8,128)S(1)} %get-tuple-element.14.c_ref, ...), custom_call_target="tpu_custom_call" | custom-call | tf_op jit(solution)/shard_map/write_out/pallas_call | solution.py:627
